TPU v7x, 32 devices: a whole 2x2x4 slice. The times are simulated.
32 devices in a mesh: parts: 2 (over y), tensor: 4 (over z), fsdp: 4 (over x, core).
Axes of the slice: x: 2, y: 2, z: 4, core: 2. Of those that a mesh axis runs over, the one named last changes fastest.
Arguments:
- tokens: bfloat16 [1024, 4096], P(('parts', 'fsdp'), 'tensor'), parts along dimension 0, may hold values from -6 to 6
- cotangent: bfloat16 [1024, 4096], P(('parts', 'fsdp'), 'tensor'), parts along dimension 0, may hold values from -6 to 6
- gate_values: bfloat16 [8, 160, 128, 128], P('fsdp', 'tensor'), may hold values from -0.1875 to 0.1875
- gate_rows: int32 [8, 160], P('fsdp', 'tensor'), may hold values from 0 to 31, as said below
- gate_scale: bfloat16 [8, 160], P('fsdp', 'tensor'), may hold values from 0.5 to 2
- up_values: bfloat16 [8, 160, 128, 128], P('fsdp', 'tensor'), may hold values from -0.1875 to 0.1875
- up_rows: int32 [8, 160], P('fsdp', 'tensor'), may hold values from 0 to 31, as said below
- up_scale: bfloat16 [8, 160], P('fsdp', 'tensor'), may hold values from 0.5 to 2
- down_values: bfloat16 [8, 160, 128, 128], P('fsdp', 'tensor'), may hold values from -0.078125 to 0.078125
- down_cols: int32 [8, 160], P('fsdp', 'tensor'), may hold values from 0 to 31, as said below
- down_scale: bfloat16 [8, 160], P('fsdp', 'tensor'), may hold values from 0.5 to 2
Outputs:
- layer_out: bfloat16 [1024, 4096], P(('parts', 'fsdp'), 'tensor'), parts along dimension 0
- grad_tokens: bfloat16 [1024, 4096], P(('parts', 'fsdp'), 'tensor'), parts along dimension 0
- grad_gate: bfloat16 [16, 160, 128, 128], P(('parts', 'fsdp'), 'tensor'), parts along dimension 0
- grad_up: bfloat16 [16, 160, 128, 128], P(('parts', 'fsdp'), 'tensor'), parts along dimension 0
- grad_down: bfloat16 [16, 160, 128, 128], P(('parts', 'fsdp'), 'tensor'), parts along dimension 0
There are 2 independent parts, one for each index of `parts`. A program takes and returns all parts, laid end to end along the dimension named above; an argument that names none is the same for every part. Nothing has to cross between parts.
Inputs may be any that keep to these rules, and one draw needn't show every extreme that they name: `gate_rows`: the 8 entries of each column name distinct input blocks; some input blocks are named far more often than others. `up_rows`: the 8 entries of each column name distinct input blocks; some input blocks are named far more often than others. `down_cols`: the 8 entries of each column name distinct output blocks; some output blocks are named far more often than others.
All inputs are finite; a program needn't handle non-finite values.
Results may differ from a plain program's by a relative error of at most 0.023.
Values may be sent and summed in bfloat16 or wider, within the bound.
A program may use at most 192 MiB of HBM per device.

v0:
```python
import jax
import jax.numpy as jnp
from jax import lax
from jax.sharding import PartitionSpec as P


def scaled_sum(products, factors):
    return jnp.sum(products * factors.astype(jnp.float32)[None, :, :, None], axis=1)


def slot_term(selected, grads, factors):
    return (
        jnp.einsum("tkra,trb->krab", selected, grads, preferred_element_type=jnp.float32)
        * factors[:, :, None, None]
    )


def local(
    tokens,
    cotangent,
    gate_values,
    gate_rows,
    gate_scale,
    up_values,
    up_rows,
    up_scale,
    down_values,
    down_cols,
    down_scale,
):
    block_size = gate_values.shape[-1]
    token_count = tokens.shape[0]
    tensor_count = lax.axis_size("tensor")
    nblocks = tokens.shape[1] * tensor_count // block_size
    local_blocks = nblocks // tensor_count
    gathered = lax.all_gather(tokens, "tensor", axis=1, tiled=True)
    x_blocks = gathered.reshape(token_count, nblocks, block_size)
    gate_where, up_where, down_where = (
        lax.all_gather(gate_rows, "fsdp", axis=0, tiled=True),
        lax.all_gather(up_rows, "fsdp", axis=0, tiled=True),
        lax.all_gather(down_cols, "fsdp", axis=0, tiled=True),
    )
    gate_blocks, gate_factor, up_blocks, up_factor, down_blocks, down_factor = (
        lax.all_gather(gate_values, "fsdp", axis=0, tiled=True),
        lax.all_gather(gate_scale, "fsdp", axis=0, tiled=True),
        lax.all_gather(up_values, "fsdp", axis=0, tiled=True),
        lax.all_gather(up_scale, "fsdp", axis=0, tiled=True),
        lax.all_gather(down_values, "fsdp", axis=0, tiled=True),
        lax.all_gather(down_scale, "fsdp", axis=0, tiled=True),
    )
    gate_sel = x_blocks[:, gate_where]
    up_sel = x_blocks[:, up_where]
    gate_pre = scaled_sum(
        jnp.einsum("tkra,krab->tkrb", gate_sel, gate_blocks, preferred_element_type=jnp.float32),
        gate_factor,
    )
    up_pre = scaled_sum(
        jnp.einsum("tkra,krab->tkrb", up_sel, up_blocks, preferred_element_type=jnp.float32),
        up_factor,
    )
    sigmoid_gate = jax.nn.sigmoid(gate_pre)
    activated = gate_pre * sigmoid_gate
    hidden = (activated * up_pre).astype(jnp.bfloat16)
    down_float = down_factor.astype(jnp.float32)
    down_scaled = (
        jnp.einsum("trb,krbc->krtc", hidden, down_blocks, preferred_element_type=jnp.float32)
        * down_float[:, :, None, None]
    )
    out_full = (
        jnp.zeros((nblocks, token_count, block_size), jnp.float32).at[down_where].add(down_scaled)
    )
    out_part = lax.psum_scatter(
        out_full.astype(jnp.bfloat16), "tensor", scatter_dimension=0, tiled=True
    ).astype(jnp.float32)
    layer_out = (
        jnp.transpose(out_part, (1, 0, 2))
        .reshape(token_count, local_blocks * block_size)
        .astype(jnp.bfloat16)
    )
    grad_full = lax.all_gather(cotangent, "tensor", axis=1, tiled=True).reshape(
        token_count, nblocks, block_size
    )
    down_sel = grad_full[:, down_where]
    gate_float = gate_factor.astype(jnp.float32)
    up_float = up_factor.astype(jnp.float32)
    grad_hidden = scaled_sum(
        jnp.einsum("tkrc,krbc->tkrb", down_sel, down_blocks, preferred_element_type=jnp.float32),
        down_factor,
    )
    grad_down = lax.psum_scatter(
        (
            jnp.einsum("trb,tkrc->krbc", hidden, down_sel, preferred_element_type=jnp.float32)
            * down_float[:, :, None, None]
        ).astype(jnp.bfloat16),
        "fsdp",
        scatter_dimension=0,
        tiled=True,
    )
    grad_gate_act = (
        grad_hidden * up_pre * sigmoid_gate * (1.0 + gate_pre * (1.0 - sigmoid_gate))
    ).astype(jnp.bfloat16)
    grad_up_act = (grad_hidden * activated).astype(jnp.bfloat16)
    grad_gate = lax.psum_scatter(
        slot_term(gate_sel, grad_gate_act, gate_float).astype(jnp.bfloat16),
        "fsdp",
        scatter_dimension=0,
        tiled=True,
    )
    grad_up = lax.psum_scatter(
        slot_term(up_sel, grad_up_act, up_float).astype(jnp.bfloat16),
        "fsdp",
        scatter_dimension=0,
        tiled=True,
    )
    back_gate = (
        jnp.einsum("trb,krab->krta", grad_gate_act, gate_blocks, preferred_element_type=jnp.float32)
        * gate_float[:, :, None, None]
    )
    back_up = (
        jnp.einsum("trb,krab->krta", grad_up_act, up_blocks, preferred_element_type=jnp.float32)
        * up_float[:, :, None, None]
    )
    in_full = (
        jnp.zeros((nblocks, token_count, block_size), jnp.float32)
        .at[gate_where]
        .add(back_gate)
        .at[up_where]
        .add(back_up)
    )
    in_part = lax.psum_scatter(
        in_full.astype(jnp.bfloat16), "tensor", scatter_dimension=0, tiled=True
    ).astype(jnp.float32)
    grad_tokens = (
        jnp.transpose(in_part, (1, 0, 2))
        .reshape(token_count, local_blocks * block_size)
        .astype(jnp.bfloat16)
    )
    return (layer_out, grad_tokens, grad_gate, grad_up, grad_down)


def solution(mesh):
    in_specs = (
        P(("parts", "fsdp"), "tensor"),
        P(("parts", "fsdp"), "tensor"),
        P("fsdp", "tensor", None, None),
        P("fsdp", "tensor"),
        P("fsdp", "tensor"),
        P("fsdp", "tensor", None, None),
        P("fsdp", "tensor"),
        P("fsdp", "tensor"),
        P("fsdp", "tensor", None, None),
        P("fsdp", "tensor"),
        P("fsdp", "tensor"),
    )
    out_specs = (
        P(("parts", "fsdp"), "tensor"),
        P(("parts", "fsdp"), "tensor"),
        P(("parts", "fsdp"), "tensor", None, None),
        P(("parts", "fsdp"), "tensor", None, None),
        P(("parts", "fsdp"), "tensor", None, None),
    )
    return jax.shard_map(local, mesh=mesh, in_specs=in_specs, out_specs=out_specs, check_vma=False)
```

profile of v0, /device:TPU:0, one launch (start us, length us, event | category | flops | bytes accessed | tf_op | source)
XLA Modules:
  0.0 881.0 jit_solution(15714218218693129327)
XLA Ops:
  7.2 0.0 all-gather.12.cloned.1.call-start
  7.3 1.8 copy.72
  9.1 0.0 all-gather.20.cloned.1.call-start
  9.1 1.8 copy.79
  11.0 0.0 all-gather.16.cloned.1.call-start
  11.0 0.7 all-gather.16.cloned.1.call-update
  11.7 0.0 all-gather.18.cloned.1.call-start
  11.7 3.6 copy.75
  15.3 0.0 all-gather.14.cloned.1.call-start
  15.4 0.5 all-gather.14.cloned.1.call-update
  15.9 0.0 reduce-scatter.8.cloned.1.call-start
  16.0 6.0 all-gather.2
  22.0 5.4 all-gather.4
  27.4 5.1 all-gather.1
  32.4 0.1 reshape.30
  32.5 5.1 all-gather.3
  37.6 0.1 reshape.38
  37.7 5.1 all-gather
  42.7 0.1 reshape.54
  42.8 5.1 all-gather.5
  47.9 0.1 copy.76
  48.0 1.6 copy.73
  49.7 20.9 %all-gather.20.cloned.1.call-done = bf16[128,4096]{0,1:T(8,128)(2,1)} async-done(((bf16[128,1024]{0,1:T(8,128)(2,1)}), bf16[128,4096]{0,1:T(8,128)(2,1)}) %all-gather.20.cloned.1.call-update) | async-done | bytes 1048592 | tf_op jit(solution)/shard_map/all_gather | solution.py:80
  70.5 1.6 copy.80
  72.1 11.2 %gather_fusion.1 = bf16[320,128,128]{2,1,0:T(8,128)(2,1)} fusion(bf16[128,32,128]{2,0,1:T(8,128)(2,1)S(1)} %copy.73, s32[1024]{0:T(1024)S(1)} %pad_clamp_fusion.1), kind=kCustom, calls=%fused_computation.1 | custom fusion | bytes 20972800 | tf_op jit(solution)/shard_map/gather | solution.py:52
  83.4 10.6 %gather_fusion = bf16[320,128,128]{2,1,0:T(8,128)(2,1)} fusion(bf16[128,32,128]{2,0,1:T(8,128)(2,1)S(1)} %copy.73, s32[1024]{0:T(1024)S(1)} %pad_clamp_fusion.2), kind=kCustom, calls=%fused_computation | custom fusion | bytes 20972800 | tf_op jit(solution)/shard_map/gather | solution.py:51
  93.9 10.7 %gather_fusion.2 = bf16[320,128,128]{2,1,0:T(8,128)(2,1)} fusion(bf16[128,32,128]{2,0,1:T(8,128)(2,1)S(1)} %copy.80, s32[1024]{0:T(1024)S(1)} %pad_clamp_fusion), kind=kCustom, calls=%fused_computation.2 | custom fusion | bytes 20972800 | tf_op jit(solution)/shard_map/gather | solution.py:83
  104.6 37.0 %all-gather.16.cloned.1.call-done = bf16[8,40,128,128]{3,2,1,0:T(8,128)(2,1)} async-done(((bf16[2,40,128,128]{3,2,1,0:T(8,128)(2,1)}), bf16[8,40,128,128]{3,2,1,0:T(8,128)(2,1)}) %all-gather.16.cloned.1.call-update) | async-done | bytes 10485776 | tf_op jit(solution)/shard_map/all_gather | solution.py:46
  141.6 10.3 %multiply_reduce_fusion.1 = f32[40,128,128]{2,1,0:T(8,128)} fusion(f32[8,40]{1,0:T(8,128)S(1)} %convert.1, bf16[128,8,40,128]{3,0,2,1:T(8,128)(2,1)} %bitcast.130, bf16[8,40,128,128]{3,2,1,0:T(8,128)(2,1)} %all-gather.16.cloned.1.call-done), kind=kOutput, calls=%fused_computation.16 | convolution fusion | flops 1352007680 | bytes 23594240 | tf_op jit(solution)/shard_map/tkra,krab->tkrb/dot_general | solution.py:58
  151.9 61.9 %all-gather.18.cloned.1.call-done = bf16[8,40,128,128]{3,2,0,1:T(8,128)(2,1)} async-done(((bf16[2,40,128,128]{3,2,0,1:T(8,128)(2,1)}), bf16[8,40,128,128]{3,2,0,1:T(8,128)(2,1)}) %all-gather.18.cloned.1.call-update) | async-done | bytes 10485776 | tf_op jit(solution)/shard_map/all_gather | solution.py:48
  213.8 13.4 %multiply_reduce_fusion = f32[40,128,128]{2,1,0:T(8,128)} fusion(f32[8,40]{0,1:T(8,128)S(1)} %copy.76, bf16[8,40,128,128]{3,2,0,1:T(8,128)(2,1)} %all-gather.18.cloned.1.call-done, bf16[128,8,40,128]{3,0,2,1:T(8,128)(2,1)} %bitcast.136), kind=kOutput, calls=%fused_computation.15 | convolution fusion | flops 1352007680 | bytes 23594240 | tf_op jit(solution)/shard_map/tkrc,krbc->tkrb/dot_general | solution.py:87
  227.2 58.2 %all-gather.14.cloned.1.call-done = bf16[8,40,128,128]{3,2,1,0:T(8,128)(2,1)} async-done(((bf16[2,40,128,128]{3,2,1,0:T(8,128)(2,1)}), bf16[8,40,128,128]{3,2,1,0:T(8,128)(2,1)}) %all-gather.14.cloned.1.call-update) | async-done | bytes 10485776 | tf_op jit(solution)/shard_map/all_gather | solution.py:44
  285.4 10.5 %multiply_reduce_fusion.2 = f32[40,128,128]{2,1,0:T(8,128)} fusion(f32[8,40]{1,0:T(8,128)S(1)} %convert, bf16[128,8,40,128]{3,0,2,1:T(8,128)(2,1)} %bitcast.132, bf16[8,40,128,128]{3,2,1,0:T(8,128)(2,1)} %all-gather.14.cloned.1.call-done), kind=kOutput, calls=%fused_computation.17 | convolution fusion | flops 1352007680 | bytes 23594240 | tf_op jit(solution)/shard_map/tkra,krab->tkrb/dot_general | solution.py:54
  296.0 5.5 fusion.21
  301.5 8.5 bitcast_multiply_fusion.5
  310.0 16.1 %copy.77 = f32[8,40,128,128]{3,2,1,0:T(8,128)} copy(f32[8,40,128,128]{3,2,0,1:T(8,128)} %bitcast_multiply_fusion.5) | data formatting | bytes 41943040 | tf_op jit(solution)/shard_map/mul | solution.py:66
  326.1 0.2 broadcast.21.clone
  326.4 41.9 %scatter_fusion = f32[32,128,128]{2,1,0:T(8,128)S(1)} fusion(f32[32,128,128]{2,1,0:T(8,128)S(1)} %broadcast.21.clone, s32[320]{0:T(512)S(1)} %reshape.54, f32[320,128,128]{2,1,0:T(8,128)} %bitcast.129), kind=kCustom, calls=%fused_computation.3 | custom fusion | flops 5242880 | bytes 62915840 | tf_op jit(solution)/shard_map/scatter-add | solution.py:70
  368.3 1.1 convert_element_type.56
  369.5 0.3 reduce-scatter.10.cloned.1.call-start
  369.7 14.3 %bitcast_multiply_fusion.4 = f32[8,40,128,128]{3,2,1,0:T(8,128)} fusion(f32[8,40]{1,0:T(8,128)S(1)} %convert, bf16[8,40,128,128]{3,2,1,0:T(8,128)(2,1)} %all-gather.14.cloned.1.call-done, bf16[128,40,128]{2,0,1:T(8,128)(2,1)} %get-tuple-element.26), kind=kOutput, calls=%fused_computation.13 | convolution fusion | flops 1347420160 | bytes 32769280 | tf_op jit(solution)/shard_map/trb,krab->krta/dot_general | solution.py:116
  384.0 0.2 broadcast.21.clone.1
  384.2 41.9 %scatter_fusion.1 = f32[32,128,128]{2,1,0:T(8,128)S(1)} fusion(f32[32,128,128]{2,1,0:T(8,128)S(1)} %broadcast.21.clone.1, s32[320]{0:T(512)S(1)} %reshape.30, f32[320,128,128]{2,1,0:T(8,128)} %bitcast.127), kind=kCustom, calls=%fused_computation.4 | custom fusion | flops 5242880 | bytes 62915840 | tf_op jit(solution)/shard_map/scatter-add | solution.py:126
  426.2 13.9 %bitcast_multiply_fusion.3 = f32[8,40,128,128]{3,2,1,0:T(8,128)} fusion(f32[8,40]{1,0:T(8,128)S(1)} %convert.1, bf16[128,40,128,1]{2,0,1,3:T(8,128)(2,1)S(1)} %get-tuple-element.25, bf16[8,40,128,128]{3,2,1,0:T(8,128)(2,1)} %all-gather.16.cloned.1.call-done), kind=kOutput, calls=%fused_computation.12 | convolution fusion | flops 1347420160 | bytes 32769280 | tf_op jit(solution)/shard_map/trb,krab->krta/dot_general | solution.py:120
  440.1 41.9 %scatter_fusion.2 = f32[32,128,128]{2,1,0:T(8,128)S(1)} fusion(f32[32,128,128]{2,1,0:T(8,128)S(1)} %scatter_fusion.1, s32[320]{0:T(512)S(1)} %reshape.38, f32[320,128,128]{2,1,0:T(8,128)} %bitcast.128), kind=kCustom, calls=%fused_computation.5 | custom fusion | flops 5242880 | bytes 62915840 | tf_op jit(solution)/shard_map/scatter-add | solution.py:128
  482.0 1.2 convert_element_type.61
  483.2 0.0 all-reduce.3.cloned.1.call-start
  483.2 9.0 %fusion = bf16[8,40,128,128]{3,2,0,1:T(8,128)(2,1)} fusion(f32[8,40]{0,1:T(8,128)S(1)} %copy.76, bf16[128,40,128,1]{2,0,3,1:T(8,128)(2,1)} %copy-done.1, bf16[128,8,40,128]{3,0,2,1:T(8,128)(2,1)} %bitcast.137), kind=kOutput, calls=%fused_computation.7 | convolution fusion | flops 1352663040 | bytes 22283520 | tf_op jit(solution)/shard_map/trb,tkrc->krbc/dot_general | solution.py:92
  492.2 0.3 reduce-scatter.12.cloned.1.call-start
  492.5 1.0 copy-done
  493.5 9.5 %fusion.2 = bf16[8,40,128,128]{3,2,1,0:T(8,128)(2,1)} fusion(f32[8,40]{1,0:T(8,128)S(1)} %convert, bf16[128,8,40,128]{3,0,2,1:T(8,128)(2,1)} %bitcast.133, bf16[128,40,128]{2,0,1:T(8,128)(2,1)S(1)} %copy-done), kind=kOutput, calls=%fused_computation.11 | convolution fusion | flops 1352663040 | bytes 22283520 | tf_op jit(solution)/shard_map/tkra,trb->krab/dot_general | solution.py:13
  503.0 0.0 reduce-scatter.14.cloned.1.call-start
  503.0 9.5 %fusion.1 = bf16[8,40,128,128]{3,2,1,0:T(8,128)(2,1)} fusion(f32[8,40]{1,0:T(8,128)S(1)} %convert.1, bf16[128,40,128,1]{2,0,1,3:T(8,128)(2,1)S(1)} %get-tuple-element.25, bf16[128,8,40,128]{3,0,2,1:T(8,128)(2,1)} %bitcast.131), kind=kOutput, calls=%fused_computation.9 | convolution fusion | flops 1352663040 | bytes 22283520 | tf_op jit(solution)/shard_map/tkra,trb->krab/dot_general | solution.py:13
  512.6 0.6 copy-done.9
  513.2 0.6 dynamic-slice
  514.4 1.1 copy.78
  515.6 0.9 copy.90
  516.4 1.2 copy.83
  517.6 0.9 copy.91
  518.5 180.0 %all-reduce.3.cloned.1.call-done = bf16[8,40,128,128]{3,2,0,1:T(8,128)(2,1)} async-done(((bf16[8,40,128,128]{3,2,0,1:T(8,128)(2,1)}), bf16[8,40,128,128]{3,2,0,1:T(8,128)(2,1)}) %all-reduce.3.cloned.1.call-update) | async-done | bytes 10485776
  698.5 2.1 constant_dynamic-slice_fusion
  700.5 1.8 copy.92
  702.3 83.9 %reduce-scatter.12.cloned.1.call-done = bf16[2,40,128,128]{3,2,1,0:T(8,128)(2,1)} async-done(((bf16[8,40,128,128]{3,2,1,0:T(8,128)(2,1)}), bf16[2,40,128,128]{3,2,1,0:T(8,128)(2,1)}) %reduce-scatter.12.cloned.1.call-update) | async-done | bytes 2621456 | tf_op jit(solution)/shard_map/reduce_scatter | solution.py:103
  786.3 87.4 %reduce-scatter.14.cloned.1.call-done = bf16[2,40,128,128]{3,2,1,0:T(8,128)(2,1)} async-done(((bf16[8,40,128,128]{3,2,1,0:T(8,128)(2,1)}), bf16[2,40,128,128]{3,2,1,0:T(8,128)(2,1)}) %reduce-scatter.14.cloned.1.call-update) | async-done | bytes 2621456 | tf_op jit(solution)/shard_map/reduce_scatter | solution.py:109
  (44 shorter events, 0.3 us)
Async XLA Ops:
  7.2 8.8 copy-start.6
  7.2 14.8 %copy-start.7 = (bf16[2,40]{1,0:T(2,128)(2,1)S(1)}, bf16[2,40]{1,0:T(2,128)(2,1)}, u32[]{:S(2)}) copy-start(bf16[2,40]{1,0:T(2,128)(2,1)} %param.18) | copy-start | bytes 484
  7.2 20.2 %copy-start.3 = (s32[2,40]{1,0:T(2,128)S(1)}, s32[2,40]{1,0:T(2,128)}, u32[]{:S(2)}) copy-start(s32[2,40]{1,0:T(2,128)} %param.14) | copy-start | bytes 964
  7.2 25.3 %copy-start.4 = (s32[2,40]{1,0:T(2,128)S(1)}, s32[2,40]{1,0:T(2,128)}, u32[]{:S(2)}) copy-start(s32[2,40]{1,0:T(2,128)} %param.17) | copy-start | bytes 964
  7.2 30.5 %copy-start.5 = (s32[2,40]{1,0:T(2,128)S(1)}, s32[2,40]{1,0:T(2,128)}, u32[]{:S(2)}) copy-start(s32[2,40]{1,0:T(2,128)} %param.20) | copy-start | bytes 964
  7.2 35.6 %copy-start.8 = (bf16[2,40]{1,0:T(2,128)(2,1)S(1)}, bf16[2,40]{1,0:T(2,128)(2,1)}, u32[]{:S(2)}) copy-start(bf16[2,40]{1,0:T(2,128)(2,1)} %param.21) | copy-start | bytes 484
  7.2 40.8 %all-gather.12.cloned.1.call-start = ((), (), s32[]{:S(2)}) async-start(), calls=%async_computation.4 | async-start | bytes 1310720 | tf_op jit(solution)/shard_map/all_gather | solution.py:36
  9.1 61.4 %all-gather.20.cloned.1.call-start = ((), (), s32[]{:S(2)}) async-start(), calls=%async_computation.9 | async-start | bytes 1310720 | tf_op jit(solution)/shard_map/all_gather | solution.py:80
  11.0 130.7 %all-gather.16.cloned.1.call-start = ((), (), s32[]{:S(2)}) async-start(), calls=%async_computation.6 | async-start | bytes 13107200 | tf_op jit(solution)/shard_map/all_gather | solution.py:46
  11.7 202.1 %all-gather.18.cloned.1.call-start = ((), (), s32[]{:S(2)}) async-start(), calls=%async_computation.7 | async-start | bytes 13107200 | tf_op jit(solution)/shard_map/all_gather | solution.py:48
  15.3 270.1 %all-gather.14.cloned.1.call-start = ((), (), s32[]{:S(2)}) async-start(), calls=%async_computation.5 | async-start | bytes 13107200 | tf_op jit(solution)/shard_map/all_gather | solution.py:44
  15.9 498.5 %reduce-scatter.8.cloned.1.call-start = ((), (), s32[]{:S(2)}) async-start(), calls=%async_computation.8 | async-start | bytes 1310720 | tf_op jit(solution)/shard_map/reduce_scatter | solution.py:72
  285.4 16.0 %slice-start = ((s8[10485760]{0:T(1024)(128)(4,1)}), s8[4194304]{0:T(1024)(128)(4,1)S(1)}, s32[]{:S(2)}) async-start(s8[10485760]{0:T(1024)(128)(4,1)} %bitcast.134), calls=%async_computation.14 | async-start | bytes 8388608
  285.4 10.5 %copy-start.2 = (f32[40,128,128]{2,1,0:T(8,128)S(1)}, f32[40,128,128]{2,1,0:T(8,128)}, u32[]{:S(2)}) copy-start(f32[40,128,128]{2,1,0:T(8,128)} %multiply_reduce_fusion.1) | copy-start | bytes 7864324
  285.4 16.0 %slice-start.1 = ((s8[10485760]{0:T(1024)(128)(4,1)}), s8[4194304]{0:T(1024)(128)(4,1)S(1)}, s32[]{:S(2)}) async-start(s8[10485760]{0:T(1024)(128)(4,1)} %bitcast.134), calls=%async_computation.15 | async-start | bytes 8388608
  285.4 16.0 %slice-start.2 = ((s8[10485760]{0:T(1024)(128)(4,1)}), s8[2097152]{0:T(1024)(128)(4,1)S(1)}, s32[]{:S(2)}) async-start(s8[10485760]{0:T(1024)(128)(4,1)} %bitcast.134), calls=%async_computation.16 | async-start | bytes 4194304
  301.5 8.6 copy-start.1
  369.5 147.0 %reduce-scatter.10.cloned.1.call-start = ((), (), s32[]{:S(2)}) async-start(), calls=%async_computation.10 | async-start | bytes 1310720 | tf_op jit(solution)/shard_map/reduce_scatter | solution.py:130
  483.2 215.3 %all-reduce.3.cloned.1.call-start = ((), (), s32[]{:S(2)}) async-start(), calls=%async_computation.13 | async-start | bytes 20971520
  492.2 1.3 copy-start
  492.2 294.0 %reduce-scatter.12.cloned.1.call-start = ((), (), s32[]{:S(2)}) async-start(), calls=%async_computation.11 | async-start | bytes 13107200 | tf_op jit(solution)/shard_map/reduce_scatter | solution.py:103
  503.0 370.7 %reduce-scatter.14.cloned.1.call-start = ((), (), s32[]{:S(2)}) async-start(), calls=%async_computation.12 | async-start | bytes 13107200 | tf_op jit(solution)/shard_map/reduce_scatter | solution.py:109
  512.5 0.7 copy-start.9
Sparse Core Ops, SparseCore 0:
  10.2 30.6 all-gather.11
  43.1 27.4 all-gather.19
  72.1 69.4 all-gather.15
  143.6 70.1 all-gather.17
  215.2 70.1 all-gather.13
  369.6 27.3 reduce-scatter.7
  483.3 27.3 reduce-scatter.9
  513.2 185.2 all-reduce.2
  701.6 84.5 reduce-scatter.11
  789.3 84.3 reduce-scatter.13
where the time goes:
time: 892 us; the launch traced here: 881 us
  waiting for transfers between devices  531 us (60%)
  other arithmetic  134 us (15%)
  matrix products  98.8 us (11%)
  local copies, waits for them, and re-layouts  69.9 us (8%)
  blocking collectives  31.6 us (4%)
  between operations  15.5 us (2%)
    unnamed x11, waiting for transfers between devices  181 us
    reduce_scatter x1, waiting for transfers between devices, local(): lax.psum_scatter(slot_term(up_sel, grad_up_act, up_float).astype(jnp.bflo...  87.4 us
    reduce_scatter x1, waiting for transfers between devices, local(): lax.psum_scatter(slot_term(gate_sel, grad_gate_act, gate_float).astype(jn...  83.9 us
    scatter-add x2, other arithmetic, local(): in_full = jnp.zeros((nblocks, token_count, block_size), jnp.float32).at[g...  83.9 us
    all_gather x1, waiting for transfers between devices, local(): lax.all_gather(down_values, 'fsdp', axis=0, tiled=True)  61.9 us
    all_gather x1, waiting for transfers between devices, local(): lax.all_gather(gate_values, 'fsdp', axis=0, tiled=True)  58.2 us
    scatter-add x1, other arithmetic, local(): jnp.zeros((nblocks, token_count, block_size), jnp.float32).at[down_where]  41.9 us
    all_gather x1, waiting for transfers between devices, local(): lax.all_gather(up_values, 'fsdp', axis=0, tiled=True)  37 us
  transfers between devices with their start and end apart: 10, of which 7 were waited for; matrix products, arithmetic and copies ran while one was open for 24% of the time, Pallas kernels for 0%

commit v1 on v0

--- a/solution.py
+++ b/solution.py
@@ -1,6 +1,10 @@
+import functools
+
 import jax
 import jax.numpy as jnp
 from jax import lax
+from jax.experimental import pallas as pl
+from jax.experimental.pallas import tpu as pltpu
 from jax.sharding import PartitionSpec as P
 
 
@@ -15,7 +19,7 @@
     )
 
 
-def local(
+def gathered_plan(
     tokens,
     cotangent,
     gate_values,
@@ -138,7 +142,205 @@
     return (layer_out, grad_tokens, grad_gate, grad_up, grad_down)
 
 
+def column_kernel(
+    shape,
+    rows_ref,
+    scale_ref,
+    near_ref,
+    far_ref,
+    *refs,
+):
+    slots, per_dev, nblk, blk, tok = shape
+    nsrc = slots // per_dev
+    weight_refs = [refs[i * nsrc : (i + 1) * nsrc] for i in range(3)]
+    grad_refs = [refs[(3 + i) * nsrc : (4 + i) * nsrc] for i in range(3)]
+    own_ref, other_ref = refs[6 * nsrc : 6 * nsrc + 2]
+    (out_acc, in_acc, gate_sel, up_sel, down_sel, gate_w, up_w, down_w) = refs[6 * nsrc + 2 :]
+    r = pl.program_id(0)
+    per_shard = near_ref.shape[3]
+
+    @pl.when(r == 0)
+    def _():
+        out_acc[...] = jnp.zeros_like(out_acc)
+        in_acc[...] = jnp.zeros_like(in_acc)
+
+    def load(which, slot, array, sel):
+        place = rows_ref[array, slot, r]
+        shard, block = place // per_shard, place % per_shard
+        lanes = slice(slot * blk, (slot + 1) * blk)
+        for c, ref in enumerate((near_ref, far_ref)):
+            for x in range(2):
+                q = c * 2 + x
+                sel[q * tok : (q + 1) * tok, lanes] = ref[shard, x, which, block]
+
+    def scaled(array, slot):
+        value = weight_refs[array][slot // per_dev][slot % per_dev, 0]
+        return (value.astype(jnp.float32) * scale_ref[array, slot, r]).astype(jnp.bfloat16)
+
+    for slot in range(slots):
+        span = slice(slot * blk, (slot + 1) * blk)
+        load(0, slot, 0, gate_sel)
+        load(0, slot, 1, up_sel)
+        load(1, slot, 2, down_sel)
+        gate_w[span, :] = scaled(0, slot)
+        up_w[span, :] = scaled(1, slot)
+        down_w[:, span] = scaled(2, slot)
+
+    nn = (((1,), (0,)), ((), ()))
+    nt = (((1,), (1,)), ((), ()))
+    dot = functools.partial(lax.dot_general, preferred_element_type=jnp.float32)
+    gate_pre = dot(gate_sel[...], gate_w[...], nn)
+    up_pre = dot(up_sel[...], up_w[...], nn)
+    grad_hidden = dot(down_sel[...], down_w[...], nt)
+    sig = jax.nn.sigmoid(gate_pre)
+    act = gate_pre * sig
+    hidden = (act * up_pre).astype(jnp.bfloat16)
+    gate_act = (grad_hidden * up_pre * sig * (1.0 + gate_pre * (1.0 - sig))).astype(jnp.bfloat16)
+    up_act = (grad_hidden * act).astype(jnp.bfloat16)
+
+    for slot in range(slots):
+        span = slice(slot * blk, (slot + 1) * blk)
+        src, sub = slot // per_dev, slot % per_dev
+        g = dot(gate_sel[:, span].T, gate_act, nn) * scale_ref[0, slot, r]
+        grad_refs[0][src][sub, 0] = g.astype(jnp.bfloat16)
+        g = dot(up_sel[:, span].T, up_act, nn) * scale_ref[1, slot, r]
+        grad_refs[1][src][sub, 0] = g.astype(jnp.bfloat16)
+    hidden_t = hidden.T
+    down = dot(hidden_t, down_sel[...], nn)
+    for slot in range(slots):
+        src, sub = slot // per_dev, slot % per_dev
+        g = down[:, slot * blk : (slot + 1) * blk] * scale_ref[2, slot, r]
+        grad_refs[2][src][sub, 0] = g.astype(jnp.bfloat16)
+
+    for array, acc, left, w in ((0, in_acc, gate_act, gate_w), (1, in_acc, up_act, up_w), (2, out_acc, hidden, down_w)):
+        product = dot(left, w[...], nn if array == 2 else nt)
+        for slot in range(slots):
+            place = rows_ref[array, slot, r]
+            acc[place] += product[:, slot * blk : (slot + 1) * blk]
+
+    @pl.when(r == pl.num_programs(0) - 1)
+    def _():
+        for which, acc in enumerate((out_acc, in_acc)):
+            for c, ref in enumerate((own_ref, other_ref)):
+                for x in range(2):
+                    q = c * 2 + x
+
+                    @pl.loop(0, nblk)
+                    def _(d):
+                        ref[d // per_shard, which, x, d % per_shard] = acc[d, q * tok : (q + 1) * tok, :].astype(jnp.bfloat16)
+
+
+def columns(table_rows, table_scale, near, far, weights, own):
+    nsrc = len(weights[0])
+    per_dev, count, blk, _ = weights[0][1].shape
+    shards, _, _, per_shard, tok, _ = near.shape
+    nblk = shards * per_shard
+    slots = per_dev * nsrc
+    total = 4 * tok
+    whole = lambda a: pl.BlockSpec(a, lambda r, *_: (0,) * len(a), pipeline_mode=pl.Buffered(1))
+    block = pl.BlockSpec((per_dev, 1, blk, blk), lambda r, *_: (0, r, 0, 0))
+    piece = jax.ShapeDtypeStruct((per_dev, count, blk, blk), jnp.bfloat16)
+    out_block = (shards, 2, 2, per_shard, tok, blk)
+    bf = jnp.bfloat16
+    flops = 2 * 9 * slots * count * total * blk * blk
+    outs = pl.pallas_call(
+        functools.partial(column_kernel, (slots, per_dev, nblk, blk, tok)),
+        grid_spec=pltpu.PrefetchScalarGridSpec(
+            num_scalar_prefetch=2,
+            grid=(count,),
+            in_specs=[whole(near.shape), whole(far.shape)] + [block] * (3 * nsrc),
+            out_specs=[block] * (3 * nsrc) + [whole(out_block)] * 2,
+            scratch_shapes=[
+                pltpu.VMEM((nblk, total, blk), jnp.float32),
+                pltpu.VMEM((nblk, total, blk), jnp.float32),
+                pltpu.VMEM((total, slots * blk), bf),
+                pltpu.VMEM((total, slots * blk), bf),
+                pltpu.VMEM((total, slots * blk), bf),
+                pltpu.VMEM((slots * blk, blk), bf),
+                pltpu.VMEM((slots * blk, blk), bf),
+                pltpu.VMEM((blk, slots * blk), bf),
+            ],
+        ),
+        out_shape=[piece] * (3 * nsrc) + [jax.ShapeDtypeStruct(out_block, bf)] * 2,
+        compiler_params=pltpu.CompilerParams(vmem_limit_bytes=60 * 1024 * 1024),
+        cost_estimate=pl.CostEstimate(flops=2 * flops, bytes_accessed=40 << 20, transcendentals=0),
+    )(table_rows, table_scale, near, far, *weights[0], *weights[1], *weights[2])
+    grads = [outs[i * nsrc : (i + 1) * nsrc] for i in range(3)]
+    return grads, outs[3 * nsrc], outs[3 * nsrc + 1]
+
+
+def swap(value, flip):
+    return lax.ppermute(value, "fsdp", [(i, i ^ flip) for i in range(4)])
+
+
+def exchanged_plan(
+    tokens,
+    cotangent,
+    gate_values,
+    gate_rows,
+    gate_scale,
+    up_values,
+    up_rows,
+    up_scale,
+    down_values,
+    down_cols,
+    down_scale,
+):
+    tok, width = tokens.shape
+    per_dev, local_cols, blk, _ = gate_values.shape
+    count = local_cols // 4
+    mine = lax.axis_index("fsdp")
+    f32, bf = jnp.float32, jnp.bfloat16
+
+    both = jnp.stack([tokens, cotangent]).reshape(2, tok, width // blk, blk).transpose(0, 2, 1, 3)
+    both = jnp.stack([both, swap(both, 2)])
+    near = lax.all_gather(both, "tensor", axis=0)
+    far = swap(near, 1)
+
+    def piece(values, flip):
+        return lax.dynamic_slice_in_dim(values, (mine ^ flip) * count, count, axis=-3)
+
+    small = jnp.stack(
+        [a.astype(f32) for a in (gate_rows, up_rows, down_cols, gate_scale, up_scale, down_scale)]
+    )
+
+    def small_piece(flip):
+        return lax.dynamic_slice_in_dim(small, (mine ^ flip) * count, count, axis=2)
+
+    tables = jnp.concatenate(
+        [small_piece(0)] + [swap(small_piece(m), m) for m in (1, 2, 3)], axis=1
+    )
+    table_rows = tables[:3].astype(jnp.int32)
+    table_scale = tables[3:]
+    weights = [
+        [piece(v, 0)] + [swap(piece(v, m), m) for m in (1, 2, 3)]
+        for v in (gate_values, up_values, down_values)
+    ]
+    grads, own, other = columns(table_rows, table_scale, near, far, weights, mine)
+
+    def home(pieces):
+        result = jnp.zeros((per_dev, local_cols, blk, blk), bf)
+        for m, part in enumerate(pieces):
+            part = part if m == 0 else swap(part, m)
+            result = lax.dynamic_update_slice_in_dim(result, part, (mine ^ m) * count, axis=1)
+        return result
+
+    grad_gate, grad_up, grad_down = [home(p) for p in grads]
+    chip = (own.astype(f32) + swap(other, 1).astype(f32)).astype(bf)
+    shard = lax.psum_scatter(chip, "tensor", scatter_dimension=0, tiled=False)
+    done = (shard[:, 0].astype(f32) + swap(shard[:, 1], 2).astype(f32)).astype(bf)
+    done = done.transpose(0, 2, 1, 3).reshape(2, tok, width)
+    return (done[0], done[1], grad_gate, grad_up, grad_down)
+
+
+def choose_plan(mesh, *args):
+    shards, columns_here = mesh.shape["fsdp"], args[2].shape[1]
+    plan = exchanged_plan if shards == 4 and columns_here % shards == 0 else gathered_plan
+    return plan(*args)
+
+
 def solution(mesh):
+    plan = functools.partial(choose_plan, mesh)
     in_specs = (
         P(("parts", "fsdp"), "tensor"),
         P(("parts", "fsdp"), "tensor"),
@@ -159,4 +361,4 @@
         P(("parts", "fsdp"), "tensor", None, None),
         P(("parts", "fsdp"), "tensor", None, None),
     )
-    return jax.shard_map(local, mesh=mesh, in_specs=in_specs, out_specs=out_specs, check_vma=False)
+    return jax.shard_map(plan, mesh=mesh, in_specs=in_specs, out_specs=out_specs, check_vma=False)

time: 892 us -> 375 us (0.42); the launches traced: 881 us -> 374 us
  waiting for transfers between devices: 531 us -> 250 us
  other arithmetic: 134 us -> 7.07 us
  matrix products: 98.8 us -> 0 us
  Pallas kernels: 0 us -> 51.4 us
  local copies, waits for them, and re-layouts: 69.9 us -> 30.3 us
  blocking collectives: 31.6 us -> 0 us
  starting transfers between devices: 0.87 us -> 20.8 us
    unnamed x11 -> x2, waiting for transfers between devices: 181 us -> 0.03 us
    reduce_scatter x4 -> x1, waiting for transfers between devices: 171 us -> 39.9 us  [exchanged_plan(): shard = lax.psum_scatter(chip, 'tensor', scatter_dimension=0, tiled=False)]
    ppermute x0 -> x25, waiting for transfers between devices: none -> 128 us  [swap(): return lax.ppermute(value, 'fsdp', [(i, i ^ flip) for i in range(4)])]
    scatter-add x3 -> x0, other arithmetic: 126 us -> none  [the longest x2 83.9 us: local(): in_full = jnp.zeros((nblocks, token_count, block_size), jnp.float32).at[g...]
    dot_general x9 -> x0, matrix products: 98.8 us -> none  [the longest x2 18.9 us: slot_term(): jnp.einsum('tkra,trb->krab', selected, grads, preferred_element_type=jnp....]
    all_gather x5 -> x1, waiting for transfers between devices: 178 us -> 82.3 us  [exchanged_plan(): near = lax.all_gather(both, 'tensor', axis=0)]
    pallas_call x0 -> x1, Pallas kernels: none -> 51.4 us  [columns(): pl.pallas_call(functools.partial(column_kernel, (slots, per_dev, nblk, bl...]
    gather x3 -> x0, local copies, waits for them, and re-layouts: 32.5 us -> none  [the longest x1 11.2 us: local(): up_sel = x_blocks[:, up_where]]
  transfers between devices with their start and end apart: 10 -> 27, of which waited for: 7 -> 14; matrix products, arithmetic and copies ran while one was open for 24% -> 7% of each run, Pallas kernels for 0% -> 0%
where the time goes in v1:
time: 375 us; the launch traced here: 374 us
  waiting for transfers between devices  250 us (67%)
  Pallas kernels  51.4 us (14%)
  local copies, waits for them, and re-layouts  30.3 us (8%)
  starting transfers between devices  20.8 us (6%)
  between operations  14.4 us (4%)
  other arithmetic  7.07 us (2%)
    ppermute x25, waiting for transfers between devices, swap(): return lax.ppermute(value, 'fsdp', [(i, i ^ flip) for i in range(4)])  128 us
    all_gather x1, waiting for transfers between devices, exchanged_plan(): near = lax.all_gather(both, 'tensor', axis=0)  82.3 us
    pallas_call x1, Pallas kernels, columns(): pl.pallas_call(functools.partial(column_kernel, (slots, per_dev, nblk, bl...  51.4 us
    reduce_scatter x1, waiting for transfers between devices, exchanged_plan(): shard = lax.psum_scatter(chip, 'tensor', scatter_dimension=0, tiled=False)  39.9 us
    ppermute x25, starting transfers between devices, swap(): return lax.ppermute(value, 'fsdp', [(i, i ^ flip) for i in range(4)])  20.8 us
    dynamic_update_slice x12, local copies, waits for them, and re-layouts, home(): lax.dynamic_update_slice_in_dim(result, part, (mine ^ m) * count, axis=1)  12.5 us
  transfers between devices with their start and end apart: 27, of which 14 were waited for; matrix products, arithmetic and copies ran while one was open for 7% of the time, Pallas kernels for 0%

profile of v1, /device:TPU:0, one launch (start us, length us, event | category | flops | bytes accessed | tf_op | source)
XLA Modules:
  0.0 374.4 jit_solution(8175087394428939148)
XLA Ops:
  7.2 1.1 copy.31
  8.3 1.1 copy.32
  9.5 3.0 collective-permute-start.3
  12.6 11.9 %collective-permute-done.3 = bf16[2,8,128,128]{2,3,1,0:T(8,128)(2,1)S(1)} collective-permute-done((bf16[2,8,128,128]{2,3,1,0:T(8,128)(2,1)S(1)}, bf16[2,8,128,128]{2,3,1,0:T(8,128)(2,1)S(1)}, u32[]{:S(2)}, u32[]{:S(2)}) %collective-permute-start.3) | collective-permute-done | bytes 524320 | tf_op jit(solution)/shard_map/ppermute | solution.py:273
  24.5 0.1 pad_maximum_fusion
  24.6 1.3 copy.33
  26.0 82.3 %all-gather.3.cloned.1.call-done = bf16[8,2,8,128,128]{4,3,2,1,0:T(8,128)(2,1)} async-done(((bf16[2,2,8,128,128]{4,3,2,1,0:T(8,128)(2,1)}), bf16[8,2,8,128,128]{4,3,2,1,0:T(8,128)(2,1)}) %all-gather.3.cloned.1.call-update) | async-done | bytes 4194320 | tf_op jit(solution)/shard_map/all_gather | solution.py:297
  108.4 2.9 constant_dynamic-slice_fusion.4
  111.3 1.6 collective-permute-start.10
  113.0 0.1 constant_dynamic-slice_fusion.15
  113.1 0.6 collective-permute-start.1
  113.8 1.2 collective-permute-start.2
  115.0 1.1 constant_dynamic-slice_fusion
  116.1 1.1 constant_dynamic-slice_fusion.8
  117.2 0.4 collective-permute-start.11
  117.6 10.9 %collective-permute-done.1 = f32[6,2,10]{2,1,0:T(2,128)S(1)} collective-permute-done((f32[6,2,10]{2,1,0:T(2,128)S(1)}, f32[6,2,10]{2,1,0:T(2,128)S(1)}, u32[]{:S(2)}, u32[]{:S(2)}) %collective-permute-start.1) | collective-permute-done | bytes 512 | tf_op jit(solution)/shard_map/ppermute | solution.py:273
  128.5 1.5 collective-permute-start.12
  130.0 0.7 collective-permute-start.5
  130.7 1.5 collective-permute-start.6
  132.1 14.0 %collective-permute-done.12.refs_10_ = bf16[2,10,128,128]{3,2,1,0:T(8,128)(2,1)S(1)} collective-permute-done((bf16[2,10,128,128]{3,2,1,0:T(8,128)(2,1)S(1)}, bf16[2,10,128,128]{3,2,1,0:T(8,128)(2,1)S(1)}, u32[]{:S(2)}, u32[]{:S(2)}) %collective-permute-start.12) | collective-permute-done | bytes 655392 | tf_op jit(solution)/shard_map/ppermute | solution.py:273
  146.1 13.0 %collective-permute-done.13.refs_11_ = bf16[2,10,128,128]{3,2,1,0:T(8,128)(2,1)S(1)} collective-permute-done((bf16[2,10,128,128]{3,2,1,0:T(8,128)(2,1)S(1)}, bf16[2,10,128,128]{3,2,1,0:T(8,128)(2,1)S(1)}, u32[]{:S(2)}, u32[]{:S(2)}) %collective-permute-start.13) | collective-permute-done | bytes 655392 | tf_op jit(solution)/shard_map/ppermute | solution.py:273
  159.2 0.8 collective-permute-start.8
  160.0 1.5 collective-permute-start.9
  161.5 0.6 fusion.5
  162.1 12.1 %collective-permute-done.6.refs_2_ = bf16[2,10,128,128]{3,2,1,0:T(8,128)(2,1)S(1)} collective-permute-done((bf16[2,10,128,128]{3,2,1,0:T(8,128)(2,1)S(1)}, bf16[2,10,128,128]{3,2,1,0:T(8,128)(2,1)S(1)}, u32[]{:S(2)}, u32[]{:S(2)}) %collective-permute-start.6) | collective-permute-done | bytes 655392 | tf_op jit(solution)/shard_map/ppermute | solution.py:273
  174.2 13.0 %collective-permute-done.7.refs_3_ = bf16[2,10,128,128]{3,2,1,0:T(8,128)(2,1)S(1)} collective-permute-done((bf16[2,10,128,128]{3,2,1,0:T(8,128)(2,1)S(1)}, bf16[2,10,128,128]{3,2,1,0:T(8,128)(2,1)S(1)}, u32[]{:S(2)}, u32[]{:S(2)}) %collective-permute-start.7) | collective-permute-done | bytes 655392 | tf_op jit(solution)/shard_map/ppermute | solution.py:273
  187.2 13.3 %collective-permute-done.9.refs_6_ = bf16[2,10,128,128]{3,2,1,0:T(8,128)(2,1)S(1)} collective-permute-done((bf16[2,10,128,128]{3,2,1,0:T(8,128)(2,1)S(1)}, bf16[2,10,128,128]{3,2,1,0:T(8,128)(2,1)S(1)}, u32[]{:S(2)}, u32[]{:S(2)}) %collective-permute-start.9) | collective-permute-done | bytes 655392 | tf_op jit(solution)/shard_map/ppermute | solution.py:273
  200.6 0.8 copy-done.18
  201.5 51.4 %shard_map.146 = (bf16[2,10,128,128]{3,2,1,0:T(8,128)(2,1)}, bf16[2,10,128,128]{3,2,1,0:T(8,128)(2,1)}, bf16[2,10,128,128]{3,2,1,0:T(8,128)(2,1)}, bf16[2,10,128...) custom-call(s32[3,8,10]{2,1,0:T(8,128)} %get-tuple-element.65.rows_r, ...), custom_call_target="tpu_custom_call" | custom-call | flops 24159191040 | bytes 41943040 | tf_op jit(solution)/shard_map/pallas_call | solution.py:246
  253.0 7.4 %collective-permute-done.14 = bf16[4,2,2,8,128,128]{5,4,3,2,1,0:T(8,128)(2,1)S(1)} collective-permute-done((bf16[4,2,2,8,128,128]{5,4,3,2,1,0:T(8,128)(2,1)}, bf16[4,2,2,8,128,128]{5,4,3,2,1,0:T(8,128)(2,1)S(1)}, u32[]{:S(2)}, u32[]{:S(2)}) %collective-permute-start.14) | collective-permute-done | bytes 4194336 | tf_op jit(solution)/shard_map/ppermute | solution.py:273
  260.3 6.1 %add_convert_fusion = bf16[4,2,2,8,128,128]{5,4,3,2,1,0:T(8,128)(2,1)} fusion(bf16[4,2,2,8,128,128]{5,4,3,2,1,0:T(8,128)(2,1)S(1)} %collective-permute-done.14, bf16[4,2,2,8,128,128]{5,4,3,2,1,0:T(8,128)(2,1)} %get-tuple-element.19), kind=kLoop, calls=%fused_computation | loop fusion | flops 8388608 | bytes 12582912 | tf_op jit(solution)/shard_map/convert_element_type | solution.py:329
  266.4 0.2 collective-permute-start.22
  266.6 1.5 collective-permute-start.23
  268.1 0.3 collective-permute-start.24
  268.4 0.4 collective-permute-start.19
  268.8 1.5 collective-permute-start.20
  270.2 2.1 broadcast.3.clone.2
  272.4 1.0 constant_dynamic-update-slice_fusion.9
  273.3 2.1 broadcast.3.clone.1
  275.5 1.0 constant_dynamic-update-slice_fusion.13
  276.4 0.6 broadcast.3.clone
  277.3 1.0 constant_dynamic-update-slice_fusion.8
  278.2 6.2 %collective-permute-done.23 = bf16[2,10,128,128]{3,2,1,0:T(8,128)(2,1)S(1)} collective-permute-done((bf16[2,10,128,128]{3,2,1,0:T(8,128)(2,1)}, bf16[2,10,128,128]{3,2,1,0:T(8,128)(2,1)S(1)}, u32[]{:S(2)}, u32[]{:S(2)}) %collective-permute-start.23) | collective-permute-done | bytes 655392 | tf_op jit(solution)/shard_map/ppermute | solution.py:273
  284.5 1.0 constant_dynamic-update-slice_fusion.7
  285.4 12.2 %collective-permute-done.24 = bf16[2,10,128,128]{3,2,1,0:T(8,128)(2,1)S(1)} collective-permute-done((bf16[2,10,128,128]{3,2,1,0:T(8,128)(2,1)}, bf16[2,10,128,128]{3,2,1,0:T(8,128)(2,1)S(1)}, u32[]{:S(2)}, u32[]{:S(2)}) %collective-permute-start.24) | collective-permute-done | bytes 655392 | tf_op jit(solution)/shard_map/ppermute | solution.py:273
  297.6 1.2 collective-permute-start.17
  298.8 0.9 constant_dynamic-update-slice_fusion.6
  299.7 1.3 collective-permute-start.18
  301.0 0.9 constant_dynamic-update-slice_fusion.12
  302.0 39.9 %reduce-scatter.2.cloned.1.call-done = bf16[1,2,2,8,128,128]{5,4,3,2,1,0:T(8,128)(2,1)} async-done(((bf16[4,2,2,8,128,128]{5,4,3,2,1,0:T(8,128)(2,1)}), bf16[1,2,2,8,128,128]{5,4,3,2,1,0:T(8,128)(2,1)}) %reduce-scatter.2.cloned.1.call-update) | async-done | bytes 1048592 | tf_op jit(solution)/shard_map/reduce_scatter | solution.py:330
  341.9 1.1 slice_bitcast_fusion
  343.0 1.5 collective-permute-start.15
  344.5 0.9 constant_dynamic-update-slice_fusion.11
  345.5 2.2 constant_dynamic-update-slice_fusion.10
  347.6 1.2 constant_dynamic-update-slice_fusion.16
  348.9 1.2 constant_dynamic-update-slice_fusion.15
  350.1 3.7 collective-permute-done.18
  353.8 1.2 constant_dynamic-update-slice_fusion.14
  355.0 10.3 %collective-permute-done.15 = bf16[2,8,128,128]{3,2,1,0:T(8,128)(2,1)S(1)} collective-permute-done((bf16[2,8,128,128]{3,2,1,0:T(8,128)(2,1)S(1)}, bf16[2,8,128,128]{3,2,1,0:T(8,128)(2,1)S(1)}, u32[]{:S(2)}, u32[]{:S(2)}) %collective-permute-start.15) | collective-permute-done | bytes 524320 | tf_op jit(solution)/shard_map/ppermute | solution.py:273
  365.3 0.1 fusion.1
  365.5 0.2 copy.35
  365.7 0.9 copy.37
  366.6 0.2 copy.36
  366.7 0.9 copy.38
  (77 shorter events, 0.7 us)
Async XLA Ops:
  7.2 101.2 %all-gather.3.cloned.1.call-start = ((), (), s32[]{:S(2)}) async-start(), calls=%async_computation.2 | async-start | bytes 5242880 | tf_op jit(solution)/shard_map/all_gather | solution.py:297
  9.5 15.0 %collective-permute-start.3 = (bf16[2,8,128,128]{2,3,1,0:T(8,128)(2,1)S(1)}, bf16[2,8,128,128]{2,3,1,0:T(8,128)(2,1)S(1)}, u32[]{:S(2)}, u32[]{:S(2)}) collective-permute-start(bf16[2,8,128,128]{2,3,1,0:T(8,128)(2,1)S(1)} %get-tuple-element.63), channel_id=1, source_target_pairs={{0,2},{1,3},{2,0},{3,1},{4,6},{5,7},{6,4},{7,5},{8,10},{9,11},{10,... | collective-permute-start | bytes 1572872 | tf_op jit(solution)/shard_map/ppermute | solution.py:273
  25.9 315.9 %reduce-scatter.2.cloned.1.call-start = ((), (), s32[]{:S(2)}) async-start(), calls=%async_computation.1 | async-start | bytes 5242880 | tf_op jit(solution)/shard_map/reduce_scatter | solution.py:330
  108.3 92.3 %collective-permute-start.4 = (bf16[4,2,2,8,128,128]{5,4,3,2,1,0:T(8,128)(2,1)}, bf16[4,2,2,8,128,128]{5,4,3,2,1,0:T(8,128)(2,1)}, u32[]{:S(2)}, u32[]{:S(2)}) collective-permute-start(bf16[4,2,2,8,128,128]{5,4,3,2,1,0:T(8,128)(2,1)} %bitcast.45), channel_id=1, source_target_pairs={{0,1},{1,0},{2,3},{3,2},{4,5},{5,4},{6,7},{7,6},{8,9},{9,8},{10,11... | collective-permute-start | bytes 12582920 | tf_op jit(solution)/shard_map/ppermute | solution.py:273
  108.3 4.5 %copy-start.7 = (s32[2,40]{1,0:T(2,128)S(1)}, s32[2,40]{1,0:T(2,128)}, u32[]{:S(2)}) copy-start(s32[2,40]{1,0:T(2,128)} %param.14) | copy-start | bytes 964
  108.3 4.5 %copy-start.8 = (s32[2,40]{1,0:T(2,128)S(1)}, s32[2,40]{1,0:T(2,128)}, u32[]{:S(2)}) copy-start(s32[2,40]{1,0:T(2,128)} %param.17) | copy-start | bytes 964
  108.3 4.5 %copy-start.9 = (s32[2,40]{1,0:T(2,128)S(1)}, s32[2,40]{1,0:T(2,128)}, u32[]{:S(2)}) copy-start(s32[2,40]{1,0:T(2,128)} %param.20) | copy-start | bytes 964
  108.3 4.6 %copy-start.19 = (bf16[2,40]{1,0:T(2,128)(2,1)S(1)}, bf16[2,40]{1,0:T(2,128)(2,1)}, u32[]{:S(2)}) copy-start(bf16[2,40]{1,0:T(2,128)(2,1)} %param.15) | copy-start | bytes 484
  108.4 4.6 %copy-start.20 = (bf16[2,40]{1,0:T(2,128)(2,1)S(1)}, bf16[2,40]{1,0:T(2,128)(2,1)}, u32[]{:S(2)}) copy-start(bf16[2,40]{1,0:T(2,128)(2,1)} %param.18) | copy-start | bytes 484
  108.4 4.6 %copy-start.21 = (bf16[2,40]{1,0:T(2,128)(2,1)S(1)}, bf16[2,40]{1,0:T(2,128)(2,1)}, u32[]{:S(2)}) copy-start(bf16[2,40]{1,0:T(2,128)(2,1)} %param.21) | copy-start | bytes 484
  108.4 6.6 %copy-start = (bf16[2,40,128,128]{3,2,1,0:T(8,128)(2,1)S(1)}, bf16[2,40,128,128]{3,2,1,0:T(8,128)(2,1)}, u32[]{:S(2)}) copy-start(bf16[2,40,128,128]{3,2,1,0:T(8,128)(2,1)} %param.19) | copy-start | bytes 7864324
  111.3 18.7 %collective-permute-start.10 = (bf16[2,10,128,128]{3,2,1,0:T(8,128)(2,1)S(1)}, bf16[2,10,128,128]{3,2,1,0:T(8,128)(2,1)S(1)}, u32[]{:S(2)}, u32[]{:S(2)}) collective-permute-start(bf16[2,10,128,128]{3,2,1,0:T(8,128)(2,1)S(1)} %get-tuple-element.52), channel_id=1, source_target_pairs={{0,3},{1,2},{2,1},{3,0},{4,7},{5,6},{6,5},{7,4},{8,11},{9,10},{10,... | collective-permute-start | bytes 1966088 | tf_op jit(solution)/shard_map/ppermute | solution.py:273
  113.1 4.2 %collective-permute-start = (f32[6,2,10]{2,1,0:T(2,128)S(1)}, f32[6,2,10]{2,1,0:T(2,128)S(1)}, u32[]{:S(2)}, u32[]{:S(2)}) collective-permute-start(f32[6,2,10]{2,1,0:T(2,128)S(1)} %get-tuple-element.69), channel_id=1, source_target_pairs={{0,1},{1,0},{2,3},{3,2},{4,5},{5,4},{6,7},{7,6},{8,9},{9,8},{10,11... | collective-permute-start | bytes 1448 | tf_op jit(solution)/shard_map/ppermute | solution.py:273
  113.1 15.4 %collective-permute-start.1 = (f32[6,2,10]{2,1,0:T(2,128)S(1)}, f32[6,2,10]{2,1,0:T(2,128)S(1)}, u32[]{:S(2)}, u32[]{:S(2)}) collective-permute-start(f32[6,2,10]{2,1,0:T(2,128)S(1)} %get-tuple-element.68), channel_id=1, source_target_pairs={{0,2},{1,3},{2,0},{3,1},{4,6},{5,7},{6,4},{7,5},{8,10},{9,11},{10,... | collective-permute-start | bytes 1448 | tf_op jit(solution)/shard_map/ppermute | solution.py:273
  113.8 2.3 copy-start.1
  113.8 16.2 %collective-permute-start.2 = (f32[6,2,10]{2,1,0:T(2,128)S(1)}, f32[6,2,10]{2,1,0:T(2,128)S(1)}, u32[]{:S(2)}, u32[]{:S(2)}) collective-permute-start(f32[6,2,10]{2,1,0:T(2,128)S(1)} %get-tuple-element.67), channel_id=1, source_target_pairs={{0,3},{1,2},{2,1},{3,0},{4,7},{5,6},{6,5},{7,4},{8,11},{9,10},{10,... | collective-permute-start | bytes 1448 | tf_op jit(solution)/shard_map/ppermute | solution.py:273
  117.2 13.4 %collective-permute-start.11 = (bf16[2,10,128,128]{3,2,1,0:T(8,128)(2,1)S(1)}, bf16[2,10,128,128]{3,2,1,0:T(8,128)(2,1)S(1)}, u32[]{:S(2)}, u32[]{:S(2)}) collective-permute-start(bf16[2,10,128,128]{3,2,1,0:T(8,128)(2,1)S(1)} %get-tuple-element.49), channel_id=1, source_target_pairs={{0,1},{1,0},{2,3},{3,2},{4,5},{5,4},{6,7},{7,6},{8,9},{9,8},{10,11... | collective-permute-start | bytes 1966088 | tf_op jit(solution)/shard_map/ppermute | solution.py:273
  128.5 17.6 %collective-permute-start.12 = (bf16[2,10,128,128]{3,2,1,0:T(8,128)(2,1)S(1)}, bf16[2,10,128,128]{3,2,1,0:T(8,128)(2,1)S(1)}, u32[]{:S(2)}, u32[]{:S(2)}) collective-permute-start(bf16[2,10,128,128]{3,2,1,0:T(8,128)(2,1)S(1)} %get-tuple-element.51), channel_id=1, source_target_pairs={{0,2},{1,3},{2,0},{3,1},{4,6},{5,7},{6,4},{7,5},{8,10},{9,11},{10,... | collective-permute-start | bytes 1966088 | tf_op jit(solution)/shard_map/ppermute | solution.py:273
  130.0 29.2 %collective-permute-start.13 = (bf16[2,10,128,128]{3,2,1,0:T(8,128)(2,1)S(1)}, bf16[2,10,128,128]{3,2,1,0:T(8,128)(2,1)S(1)}, u32[]{:S(2)}, u32[]{:S(2)}) collective-permute-start(bf16[2,10,128,128]{3,2,1,0:T(8,128)(2,1)S(1)} %get-tuple-element.48), channel_id=1, source_target_pairs={{0,3},{1,2},{2,1},{3,0},{4,7},{5,6},{6,5},{7,4},{8,11},{9,10},{10,... | collective-permute-start | bytes 1966088 | tf_op jit(solution)/shard_map/ppermute | solution.py:273
  130.0 71.4 %copy-start.10 = (bf16[2,10,128,128]{3,2,1,0:T(8,128)(2,1)}, bf16[2,10,128,128]{3,2,1,0:T(8,128)(2,1)S(1)}, u32[]{:S(2)}) copy-start(bf16[2,10,128,128]{3,2,1,0:T(8,128)(2,1)S(1)} %collective-permute-done.10.refs_7_) | copy-start | bytes 1966084
  130.0 30.0 %collective-permute-start.5 = (bf16[2,10,128,128]{3,2,1,0:T(8,128)(2,1)S(1)}, bf16[2,10,128,128]{3,2,1,0:T(8,128)(2,1)S(1)}, u32[]{:S(2)}, u32[]{:S(2)}) collective-permute-start(bf16[2,10,128,128]{3,2,1,0:T(8,128)(2,1)S(1)} %get-tuple-element.57), channel_id=1, source_target_pairs={{0,1},{1,0},{2,3},{3,2},{4,5},{5,4},{6,7},{7,6},{8,9},{9,8},{10,11... | collective-permute-start | bytes 1966088 | tf_op jit(solution)/shard_map/ppermute | solution.py:273
  130.7 70.8 %copy-start.11 = (bf16[2,10,128,128]{3,2,1,0:T(8,128)(2,1)}, bf16[2,10,128,128]{3,2,1,0:T(8,128)(2,1)S(1)}, u32[]{:S(2)}) copy-start(bf16[2,10,128,128]{3,2,1,0:T(8,128)(2,1)S(1)} %collective-permute-done.11.refs_9_) | copy-start | bytes 1966084
  130.7 43.5 %collective-permute-start.6 = (bf16[2,10,128,128]{3,2,1,0:T(8,128)(2,1)S(1)}, bf16[2,10,128,128]{3,2,1,0:T(8,128)(2,1)S(1)}, u32[]{:S(2)}, u32[]{:S(2)}) collective-permute-start(bf16[2,10,128,128]{3,2,1,0:T(8,128)(2,1)S(1)} %get-tuple-element.59), channel_id=1, source_target_pairs={{0,2},{1,3},{2,0},{3,1},{4,6},{5,7},{6,4},{7,5},{8,10},{9,11},{10,... | collective-permute-start | bytes 1966088 | tf_op jit(solution)/shard_map/ppermute | solution.py:273
  146.1 55.3 %copy-start.12 = (bf16[2,10,128,128]{3,2,1,0:T(8,128)(2,1)}, bf16[2,10,128,128]{3,2,1,0:T(8,128)(2,1)S(1)}, u32[]{:S(2)}) copy-start(bf16[2,10,128,128]{3,2,1,0:T(8,128)(2,1)S(1)} %collective-permute-done.12.refs_10_) | copy-start | bytes 1966084
  146.1 41.1 %collective-permute-start.7 = (bf16[2,10,128,128]{3,2,1,0:T(8,128)(2,1)S(1)}, bf16[2,10,128,128]{3,2,1,0:T(8,128)(2,1)S(1)}, u32[]{:S(2)}, u32[]{:S(2)}) collective-permute-start(bf16[2,10,128,128]{3,2,1,0:T(8,128)(2,1)S(1)} %get-tuple-element.56), channel_id=1, source_target_pairs={{0,3},{1,2},{2,1},{3,0},{4,7},{5,6},{6,5},{7,4},{8,11},{9,10},{10,... | collective-permute-start | bytes 1966088 | tf_op jit(solution)/shard_map/ppermute | solution.py:273
  159.2 42.3 %copy-start.13 = (bf16[2,10,128,128]{3,2,1,0:T(8,128)(2,1)}, bf16[2,10,128,128]{3,2,1,0:T(8,128)(2,1)S(1)}, u32[]{:S(2)}) copy-start(bf16[2,10,128,128]{3,2,1,0:T(8,128)(2,1)S(1)} %collective-permute-done.13.refs_11_) | copy-start | bytes 1966084
  159.2 28.1 %collective-permute-start.8 = (bf16[2,10,128,128]{3,2,1,0:T(8,128)(2,1)S(1)}, bf16[2,10,128,128]{3,2,1,0:T(8,128)(2,1)S(1)}, u32[]{:S(2)}, u32[]{:S(2)}) collective-permute-start(bf16[2,10,128,128]{3,2,1,0:T(8,128)(2,1)S(1)} %get-tuple-element.53), channel_id=1, source_target_pairs={{0,1},{1,0},{2,3},{3,2},{4,5},{5,4},{6,7},{7,6},{8,9},{9,8},{10,11... | collective-permute-start | bytes 1966088 | tf_op jit(solution)/shard_map/ppermute | solution.py:273
  160.0 41.5 %copy-start.14 = (bf16[2,10,128,128]{3,2,1,0:T(8,128)(2,1)}, bf16[2,10,128,128]{3,2,1,0:T(8,128)(2,1)S(1)}, u32[]{:S(2)}) copy-start(bf16[2,10,128,128]{3,2,1,0:T(8,128)(2,1)S(1)} %collective-permute-done.5.refs_1_) | copy-start | bytes 1966084
  160.0 40.6 %collective-permute-start.9 = (bf16[2,10,128,128]{3,2,1,0:T(8,128)(2,1)S(1)}, bf16[2,10,128,128]{3,2,1,0:T(8,128)(2,1)S(1)}, u32[]{:S(2)}, u32[]{:S(2)}) collective-permute-start(bf16[2,10,128,128]{3,2,1,0:T(8,128)(2,1)S(1)} %get-tuple-element.55), channel_id=1, source_target_pairs={{0,2},{1,3},{2,0},{3,1},{4,6},{5,7},{6,4},{7,5},{8,10},{9,11},{10,... | collective-permute-start | bytes 1966088 | tf_op jit(solution)/shard_map/ppermute | solution.py:273
  174.2 27.2 %copy-start.15 = (bf16[2,10,128,128]{3,2,1,0:T(8,128)(2,1)}, bf16[2,10,128,128]{3,2,1,0:T(8,128)(2,1)S(1)}, u32[]{:S(2)}) copy-start(bf16[2,10,128,128]{3,2,1,0:T(8,128)(2,1)S(1)} %collective-permute-done.6.refs_2_) | copy-start | bytes 1966084
  187.2 13.3 %copy-start.16 = (bf16[2,10,128,128]{3,2,1,0:T(8,128)(2,1)}, bf16[2,10,128,128]{3,2,1,0:T(8,128)(2,1)S(1)}, u32[]{:S(2)}) copy-start(bf16[2,10,128,128]{3,2,1,0:T(8,128)(2,1)S(1)} %collective-permute-done.7.refs_3_) | copy-start | bytes 1966084
  187.2 13.3 %copy-start.17 = (bf16[2,10,128,128]{3,2,1,0:T(8,128)(2,1)}, bf16[2,10,128,128]{3,2,1,0:T(8,128)(2,1)S(1)}, u32[]{:S(2)}) copy-start(bf16[2,10,128,128]{3,2,1,0:T(8,128)(2,1)S(1)} %collective-permute-done.8.refs_5_) | copy-start | bytes 1966084
  200.6 0.9 copy-start.18
  252.9 7.4 %collective-permute-start.14 = (bf16[4,2,2,8,128,128]{5,4,3,2,1,0:T(8,128)(2,1)}, bf16[4,2,2,8,128,128]{5,4,3,2,1,0:T(8,128)(2,1)S(1)}, u32[]{:S(2)}, u32[]{:S(2)}) collective-permute-start(bf16[4,2,2,8,128,128]{5,4,3,2,1,0:T(8,128)(2,1)} %get-tuple-element.20), channel_id=1, source_target_pairs={{0,1},{1,0},{2,3},{3,2},{4,5},{5,4},{6,7},{7,6},{8,9},{9,8},{10,11... | collective-permute-start | bytes 12582920 | tf_op jit(solution)/shard_map/ppermute | solution.py:273
  266.4 6.0 %copy-start.6 = (bf16[2,10,128,128]{3,2,1,0:T(8,128)(2,1)S(1)}, bf16[2,10,128,128]{3,2,1,0:T(8,128)(2,1)}, u32[]{:S(2)}) copy-start(bf16[2,10,128,128]{3,2,1,0:T(8,128)(2,1)} %get-tuple-element.29) | copy-start | bytes 1966084
  266.4 10.7 %collective-permute-start.22 = (bf16[2,10,128,128]{3,2,1,0:T(8,128)(2,1)}, bf16[2,10,128,128]{3,2,1,0:T(8,128)(2,1)S(1)}, u32[]{:S(2)}, u32[]{:S(2)}) collective-permute-start(bf16[2,10,128,128]{3,2,1,0:T(8,128)(2,1)} %get-tuple-element.30), channel_id=1, source_target_pairs={{0,1},{1,0},{2,3},{3,2},{4,5},{5,4},{6,7},{7,6},{8,9},{9,8},{10,11... | collective-permute-start | bytes 1966088 | tf_op jit(solution)/shard_map/ppermute | solution.py:273
  266.6 17.8 %collective-permute-start.23 = (bf16[2,10,128,128]{3,2,1,0:T(8,128)(2,1)}, bf16[2,10,128,128]{3,2,1,0:T(8,128)(2,1)S(1)}, u32[]{:S(2)}, u32[]{:S(2)}) collective-permute-start(bf16[2,10,128,128]{3,2,1,0:T(8,128)(2,1)} %get-tuple-element.31), channel_id=1, source_target_pairs={{0,2},{1,3},{2,0},{3,1},{4,6},{5,7},{6,4},{7,5},{8,10},{9,11},{10,... | collective-permute-start | bytes 1966088 | tf_op jit(solution)/shard_map/ppermute | solution.py:273
  268.1 29.5 %collective-permute-start.24 = (bf16[2,10,128,128]{3,2,1,0:T(8,128)(2,1)}, bf16[2,10,128,128]{3,2,1,0:T(8,128)(2,1)S(1)}, u32[]{:S(2)}, u32[]{:S(2)}) collective-permute-start(bf16[2,10,128,128]{3,2,1,0:T(8,128)(2,1)} %get-tuple-element.32), channel_id=1, source_target_pairs={{0,3},{1,2},{2,1},{3,0},{4,7},{5,6},{6,5},{7,4},{8,11},{9,10},{10,... | collective-permute-start | bytes 1966088 | tf_op jit(solution)/shard_map/ppermute | solution.py:273
  268.4 31.4 %collective-permute-start.19 = (bf16[2,10,128,128]{3,2,1,0:T(8,128)(2,1)}, bf16[2,10,128,128]{3,2,1,0:T(8,128)(2,1)S(1)}, u32[]{:S(2)}, u32[]{:S(2)}) collective-permute-start(bf16[2,10,128,128]{3,2,1,0:T(8,128)(2,1)} %get-tuple-element.26), channel_id=1, source_target_pairs={{0,1},{1,0},{2,3},{3,2},{4,5},{5,4},{6,7},{7,6},{8,9},{9,8},{10,11... | collective-permute-start | bytes 1966088 | tf_op jit(solution)/shard_map/ppermute | solution.py:273
  268.8 74.2 %collective-permute-start.20 = (bf16[2,10,128,128]{3,2,1,0:T(8,128)(2,1)}, bf16[2,10,128,128]{3,2,1,0:T(8,128)(2,1)S(1)}, u32[]{:S(2)}, u32[]{:S(2)}) collective-permute-start(bf16[2,10,128,128]{3,2,1,0:T(8,128)(2,1)} %get-tuple-element.27), channel_id=1, source_target_pairs={{0,2},{1,3},{2,0},{3,1},{4,6},{5,7},{6,4},{7,5},{8,10},{9,11},{10,... | collective-permute-start | bytes 1966088 | tf_op jit(solution)/shard_map/ppermute | solution.py:273
  272.4 3.1 copy-start.5
  275.5 1.6 copy-start.4
  277.2 68.3 %collective-permute-start.21 = (bf16[2,10,128,128]{3,2,1,0:T(8,128)(2,1)}, bf16[2,10,128,128]{3,2,1,0:T(8,128)(2,1)}, u32[]{:S(2)}, u32[]{:S(2)}) collective-permute-start(bf16[2,10,128,128]{3,2,1,0:T(8,128)(2,1)} %get-tuple-element.28), channel_id=1, source_target_pairs={{0,3},{1,2},{2,1},{3,0},{4,7},{5,6},{6,5},{7,4},{8,11},{9,10},{10,... | collective-permute-start | bytes 1966088 | tf_op jit(solution)/shard_map/ppermute | solution.py:273
  284.5 63.2 %collective-permute-start.16 = (bf16[2,10,128,128]{3,2,1,0:T(8,128)(2,1)}, bf16[2,10,128,128]{3,2,1,0:T(8,128)(2,1)}, u32[]{:S(2)}, u32[]{:S(2)}) collective-permute-start(bf16[2,10,128,128]{3,2,1,0:T(8,128)(2,1)} %get-tuple-element.22), channel_id=1, source_target_pairs={{0,1},{1,0},{2,3},{3,2},{4,5},{5,4},{6,7},{7,6},{8,9},{9,8},{10,11... | collective-permute-start | bytes 1966088 | tf_op jit(solution)/shard_map/ppermute | solution.py:273
  297.6 51.3 %collective-permute-start.17 = (bf16[2,10,128,128]{3,2,1,0:T(8,128)(2,1)}, bf16[2,10,128,128]{3,2,1,0:T(8,128)(2,1)}, u32[]{:S(2)}, u32[]{:S(2)}) collective-permute-start(bf16[2,10,128,128]{3,2,1,0:T(8,128)(2,1)} %get-tuple-element.23), channel_id=1, source_target_pairs={{0,2},{1,3},{2,0},{3,1},{4,6},{5,7},{6,4},{7,5},{8,10},{9,11},{10,... | collective-permute-start | bytes 1966088 | tf_op jit(solution)/shard_map/ppermute | solution.py:273
  299.7 54.0 %collective-permute-start.18 = (bf16[2,10,128,128]{3,2,1,0:T(8,128)(2,1)}, bf16[2,10,128,128]{3,2,1,0:T(8,128)(2,1)}, u32[]{:S(2)}, u32[]{:S(2)}) collective-permute-start(bf16[2,10,128,128]{3,2,1,0:T(8,128)(2,1)} %get-tuple-element.24), channel_id=1, source_target_pairs={{0,3},{1,2},{2,1},{3,0},{4,7},{5,6},{6,5},{7,4},{8,11},{9,10},{10,... | collective-permute-start | bytes 1966088 | tf_op jit(solution)/shard_map/ppermute | solution.py:273
  343.0 22.3 %collective-permute-start.15 = (bf16[2,8,128,128]{3,2,1,0:T(8,128)(2,1)S(1)}, bf16[2,8,128,128]{3,2,1,0:T(8,128)(2,1)S(1)}, u32[]{:S(2)}, u32[]{:S(2)}) collective-permute-start(bf16[2,8,128,128]{3,2,1,0:T(8,128)(2,1)S(1)} %slice_bitcast_fusion), channel_id=1, source_target_pairs={{0,2},{1,3},{2,0},{3,1},{4,6},{5,7},{6,4},{7,5},{8,10},{9,11},{10,... | collective-permute-start | bytes 1572872 | tf_op jit(solution)/shard_map/ppermute | solution.py:273
  345.5 19.9 %copy-start.3 = (bf16[1,2,2,8,128,128]{5,4,3,2,1,0:T(8,128)(2,1)S(1)}, bf16[1,2,2,8,128,128]{5,4,3,2,1,0:T(8,128)(2,1)}, u32[]{:S(2)}) copy-start(bf16[1,2,2,8,128,128]{5,4,3,2,1,0:T(8,128)(2,1)} %reduce-scatter.2.cloned.1.call-done) | copy-start | bytes 3145732
  355.0 12.6 %copy-start.2 = (bf16[2,40,128,128]{3,2,1,0:T(8,128)(2,1)}, bf16[2,40,128,128]{3,2,1,0:T(8,128)(2,1)S(1)}, u32[]{:S(2)}) copy-start(bf16[2,40,128,128]{3,2,1,0:T(8,128)(2,1)S(1)} %constant_dynamic-update-slice_fusion.14) | copy-start | bytes 7864324
Sparse Core Ops, SparseCore 0:
  26.1 82.2 all-gather.2
  266.6 75.2 reduce-scatter.1

commit v2 on v1

--- a/solution.py
+++ b/solution.py
@@ -142,39 +142,215 @@
     return (layer_out, grad_tokens, grad_gate, grad_up, grad_down)
 
 
+SPLIT = 5
+
+
+def gather_kernel(shards, small, both, wg, wu, wd, tok_all, rg, ru, rd, table, *sems):
+    (z_send, z_recv, c_send, c_recv, x_send, x_recv, w_send, w_recv, y_send, y_recv, n_send, n_recv, s_send, s_recv, here) = sems
+    part, t, f = lax.axis_index("parts"), lax.axis_index("tensor"), lax.axis_index("fsdp")
+    flip = [f, (f // 2) * 2 + 1 - f % 2, (f + 2) % 4, ((f + 2) % 4 // 2) * 2 + 1 - f % 2]
+    count = rg.shape[2]
+    last = shards - 1
+    weights = ((wg, rg), (wu, ru), (wd, rd))
+
+    def to(where, src, dst, send, recv):
+        return pltpu.make_async_remote_copy(
+            src_ref=src, dst_ref=dst, send_sem=send, recv_sem=recv,
+            device_id=where, device_id_type=pl.DeviceIdType.MESH,
+        )
+
+    def across(m):
+        return (part, t, flip[m])
+
+    over = (1 - part, t, f)
+    ups = ((part, t + 1, f), (part, t - 1, f))
+    more = (t < last, t > 0)
+
+    barrier = pltpu.get_barrier_semaphore()
+    for m in (1, 2, 3):
+        pl.semaphore_signal(barrier, inc=1, device_id=across(m), device_id_type=pl.DeviceIdType.MESH)
+    pl.semaphore_signal(barrier, inc=1, device_id=over, device_id_type=pl.DeviceIdType.MESH)
+    for way in range(2):
+        @pl.when(more[way])
+        def _():
+            pl.semaphore_signal(barrier, inc=1, device_id=ups[way], device_id_type=pl.DeviceIdType.MESH)
+    ends = jnp.logical_or(t == 0, t == last)
+
+    @pl.when(ends)
+    def _():
+        pl.semaphore_wait(barrier, 5)
+
+    @pl.when(jnp.logical_not(ends))
+    def _():
+        pl.semaphore_wait(barrier, 6)
+
+    def z_copy(way, src, x, own=False):
+        source = both if own else tok_all.at[0, src, x]
+        return to(ups[way], source, tok_all.at[0, src, x], z_send.at[way, src, x], z_recv.at[way, src, x])
+
+    def c_copy(src, x, own=False):
+        source = both if own else tok_all.at[0, src, x]
+        return to(across(1), source, tok_all.at[1, src, x], c_send.at[src, x], c_recv.at[src, x])
+
+    x_copy = to(across(2), both, tok_all.at[0, t, 1], x_send, x_recv)
+    keep = pltpu.make_async_copy(both, tok_all.at[0, t, 0], here)
+    x_copy.start()
+    for way in range(2):
+        @pl.when(more[way])
+        def _():
+            z_copy(way, t, 0, True).start()
+    tables = [
+        to(across(m), small.at[flip[m]], table.at[m - 1], s_send.at[m - 1], s_recv.at[m - 1])
+        for m in (1, 2, 3)
+    ]
+    for c in tables:
+        c.start()
+    c_copy(t, 0, True).start()
+    w_copies, y_copies, y_waits, n_copies = [], [], [], []
+    for w, r in weights:
+        for m in (2, 3):
+            j = len(w_copies)
+            w_copies.append(to(across(m), w.at[part, pl.ds(flip[m] * count, count)], r.at[m - 1, part], w_send.at[j], w_recv.at[j]))
+            y_copies.append(to(over, r.at[m - 1, part], r.at[m - 1, part], y_send.at[j], y_recv.at[j]))
+            y_waits.append(to(over, r.at[m - 1, part], r.at[m - 1, 1 - part], y_send.at[j], y_recv.at[j]))
+        for k in range(2):
+            j = len(n_copies)
+            n_copies.append(to(across(1), w.at[k, pl.ds(flip[1] * count, count)], r.at[0, k], n_send.at[j], n_recv.at[j]))
+    for c in w_copies:
+        c.start()
+    for c in n_copies:
+        c.start()
+    keep.start()
+
+    x_copy.wait_recv()
+    for way in range(2):
+        @pl.when(more[way])
+        def _():
+            z_copy(way, t, 1).start()
+    c_copy(t, 1).start()
+
+    def arrive(step, x):
+        for way in range(2):
+            src = t - step if way == 0 else t + step
+
+            @pl.when(src >= 0 if way == 0 else src <= last)
+            def _():
+                z_copy(way, src, x).wait_recv()
+
+                @pl.when(more[way])
+                def _():
+                    z_copy(way, src, x).start()
+
+                c_copy(src, x).start()
+
+    def relay(j):
+        w_copies[j].wait_recv()
+        y_copies[j].start()
+
+    order = [(s, x) for s in range(1, shards) for x in range(2)]
+    done = 0
+    for i, (s, x) in enumerate(order):
+        arrive(s, x)
+        while done < len(w_copies) and done < 2 * i + 1:
+            relay(done)
+            done += 1
+    while done < len(w_copies):
+        relay(done)
+        done += 1
+
+    for way in range(2):
+        for s in range(shards):
+            src = t - s if way == 0 else t + s
+
+            @pl.when(jnp.logical_and(src >= 0 if way == 0 else src <= last, more[way]))
+            def _():
+                for x in range(2):
+                    z_copy(way, src, x, s == 0 and x == 0).wait_send()
+    for src in range(shards):
+        for x in range(2):
+            c_copy(src, x).wait_send()
+            c_copy(src, x).wait_recv()
+    for c in tables + n_copies:
+        c.wait_send()
+        c.wait_recv()
+    x_copy.wait_send()
+    for c in w_copies + y_copies:
+        c.wait_send()
+    for c in y_waits:
+        c.wait_recv()
+    keep.wait()
+
+
+def gather(small, both, weights, shards):
+    per_dev, local_cols, blk, _ = weights[0].shape
+    count = local_cols // 4
+    bf = jnp.bfloat16
+    dma = lambda *a: pltpu.SemaphoreType.DMA(a)
+    received = jax.ShapeDtypeStruct((3, per_dev, count, blk, blk), bf)
+    anywhere = pl.BlockSpec(memory_space=pl.ANY)
+    z = (2, shards, 2)
+    c = (shards, 2)
+    one = pltpu.SemaphoreType.DMA
+    return pl.pallas_call(
+        functools.partial(gather_kernel, shards),
+        out_shape=[
+            jax.ShapeDtypeStruct((2, shards, 2) + both.shape, bf),
+            received, received, received,
+            jax.ShapeDtypeStruct((3,) + small.shape[1:], jnp.float32),
+        ],
+        in_specs=[anywhere] * 5,
+        out_specs=[anywhere] * 5,
+        scratch_shapes=[dma(*z), dma(*z), dma(*c), dma(*c), one, one, dma(6), dma(6), dma(6), dma(6), dma(6), dma(6), dma(3), dma(3), one],
+        compiler_params=pltpu.CompilerParams(collective_id=0, has_side_effects=True),
+    )(small, both, *weights)
+
+
 def column_kernel(
     shape,
     rows_ref,
     scale_ref,
-    near_ref,
-    far_ref,
+    mine_ref,
+    tok_ref,
     *refs,
 ):
-    slots, per_dev, nblk, blk, tok = shape
+    slots, per_dev, nblk, blk, tok, base, nprev = shape
     nsrc = slots // per_dev
-    weight_refs = [refs[i * nsrc : (i + 1) * nsrc] for i in range(3)]
-    grad_refs = [refs[(3 + i) * nsrc : (4 + i) * nsrc] for i in range(3)]
-    own_ref, other_ref = refs[6 * nsrc : 6 * nsrc + 2]
-    (out_acc, in_acc, gate_sel, up_sel, down_sel, gate_w, up_w, down_w) = refs[6 * nsrc + 2 :]
-    r = pl.program_id(0)
-    per_shard = near_ref.shape[3]
-
-    @pl.when(r == 0)
+    prev_refs, refs = refs[:nprev], refs[nprev:]
+    own_w, recv_w = refs[:3], refs[3:6]
+    grad_refs = [refs[6 + i * nsrc : 6 + (1 + i) * nsrc] for i in range(3)]
+    own_ref, other_ref = refs[3 * nsrc + 6 : 3 * nsrc + 8]
+    (out_acc, in_acc, gate_sel, up_sel, down_sel, gate_w, up_w, down_w) = refs[3 * nsrc + 8 :]
+    step = pl.program_id(0)
+    r = step + base
+    per_shard = tok_ref.shape[4]
+
+    @pl.when(step == 0)
     def _():
-        out_acc[...] = jnp.zeros_like(out_acc)
-        in_acc[...] = jnp.zeros_like(in_acc)
+        if not nprev:
+            out_acc[...] = jnp.zeros_like(out_acc)
+            in_acc[...] = jnp.zeros_like(in_acc)
+            return
+        for which, acc in enumerate((out_acc, in_acc)):
+            for c, ref in enumerate(prev_refs):
+                for x in range(2):
+                    q = c * 2 + x
+
+                    @pl.loop(0, nblk)
+                    def _(d):
+                        acc[d, q * tok : (q + 1) * tok, :] = ref[d // per_shard, which, x, d % per_shard].astype(jnp.float32)
 
     def load(which, slot, array, sel):
         place = rows_ref[array, slot, r]
         shard, block = place // per_shard, place % per_shard
         lanes = slice(slot * blk, (slot + 1) * blk)
-        for c, ref in enumerate((near_ref, far_ref)):
+        for c in range(2):
             for x in range(2):
                 q = c * 2 + x
-                sel[q * tok : (q + 1) * tok, lanes] = ref[shard, x, which, block]
+                sel[q * tok : (q + 1) * tok, lanes] = tok_ref[c, shard, x, which, block]
 
     def scaled(array, slot):
-        value = weight_refs[array][slot // per_dev][slot % per_dev, 0]
+        src, sub = slot // per_dev, slot % per_dev
+        value = recv_w[array][src - 1, sub, 0] if src else own_w[array][sub, 0]
         return (value.astype(jnp.float32) * scale_ref[array, slot, r]).astype(jnp.bfloat16)
 
     for slot in range(slots):
@@ -218,7 +394,7 @@
             place = rows_ref[array, slot, r]
             acc[place] += product[:, slot * blk : (slot + 1) * blk]
 
-    @pl.when(r == pl.num_programs(0) - 1)
+    @pl.when(step == pl.num_programs(0) - 1)
     def _():
         for which, acc in enumerate((out_acc, in_acc)):
             for c, ref in enumerate((own_ref, other_ref)):
@@ -230,25 +406,27 @@
                         ref[d // per_shard, which, x, d % per_shard] = acc[d, q * tok : (q + 1) * tok, :].astype(jnp.bfloat16)
 
 
-def columns(table_rows, table_scale, near, far, weights, own):
-    nsrc = len(weights[0])
-    per_dev, count, blk, _ = weights[0][1].shape
-    shards, _, _, per_shard, tok, _ = near.shape
+def columns(table_rows, table_scale, mine, tok_all, own_w, recv_w, base, size, prev):
+    nsrc = 1 + recv_w[0].shape[0]
+    _, per_dev, count, blk, _ = recv_w[0].shape
+    _, shards, _, _, per_shard, tok, _ = tok_all.shape
     nblk = shards * per_shard
     slots = per_dev * nsrc
     total = 4 * tok
     whole = lambda a: pl.BlockSpec(a, lambda r, *_: (0,) * len(a), pipeline_mode=pl.Buffered(1))
+    own_block = pl.BlockSpec((per_dev, 1, blk, blk), lambda r, rows, scale, at: (0, at[0] * count + base + r, 0, 0))
+    recv_block = pl.BlockSpec((nsrc - 1, per_dev, 1, blk, blk), lambda r, *_: (0, 0, base + r, 0, 0))
     block = pl.BlockSpec((per_dev, 1, blk, blk), lambda r, *_: (0, r, 0, 0))
-    piece = jax.ShapeDtypeStruct((per_dev, count, blk, blk), jnp.bfloat16)
+    piece = jax.ShapeDtypeStruct((per_dev, size, blk, blk), jnp.bfloat16)
     out_block = (shards, 2, 2, per_shard, tok, blk)
     bf = jnp.bfloat16
-    flops = 2 * 9 * slots * count * total * blk * blk
+    flops = 2 * 9 * slots * size * total * blk * blk
     outs = pl.pallas_call(
-        functools.partial(column_kernel, (slots, per_dev, nblk, blk, tok)),
+        functools.partial(column_kernel, (slots, per_dev, nblk, blk, tok, base, len(prev))),
         grid_spec=pltpu.PrefetchScalarGridSpec(
-            num_scalar_prefetch=2,
-            grid=(count,),
-            in_specs=[whole(near.shape), whole(far.shape)] + [block] * (3 * nsrc),
+            num_scalar_prefetch=3,
+            grid=(size,),
+            in_specs=[whole(tok_all.shape)] + [whole(out_block)] * len(prev) + [own_block] * 3 + [recv_block] * 3,
             out_specs=[block] * (3 * nsrc) + [whole(out_block)] * 2,
             scratch_shapes=[
                 pltpu.VMEM((nblk, total, blk), jnp.float32),
@@ -264,9 +442,9 @@
         out_shape=[piece] * (3 * nsrc) + [jax.ShapeDtypeStruct(out_block, bf)] * 2,
         compiler_params=pltpu.CompilerParams(vmem_limit_bytes=60 * 1024 * 1024),
         cost_estimate=pl.CostEstimate(flops=2 * flops, bytes_accessed=40 << 20, transcendentals=0),
-    )(table_rows, table_scale, near, far, *weights[0], *weights[1], *weights[2])
+    )(table_rows, table_scale, mine, tok_all, *prev, *own_w, *recv_w)
     grads = [outs[i * nsrc : (i + 1) * nsrc] for i in range(3)]
-    return grads, outs[3 * nsrc], outs[3 * nsrc + 1]
+    return grads, outs[3 * nsrc :]
 
 
 def swap(value, flip):
@@ -292,50 +470,46 @@
     mine = lax.axis_index("fsdp")
     f32, bf = jnp.float32, jnp.bfloat16
 
+    shards = lax.axis_size("tensor")
     both = jnp.stack([tokens, cotangent]).reshape(2, tok, width // blk, blk).transpose(0, 2, 1, 3)
-    both = jnp.stack([both, swap(both, 2)])
-    near = lax.all_gather(both, "tensor", axis=0)
-    far = swap(near, 1)
-
-    def piece(values, flip):
-        return lax.dynamic_slice_in_dim(values, (mine ^ flip) * count, count, axis=-3)
-
     small = jnp.stack(
         [a.astype(f32) for a in (gate_rows, up_rows, down_cols, gate_scale, up_scale, down_scale)]
     )
-
-    def small_piece(flip):
-        return lax.dynamic_slice_in_dim(small, (mine ^ flip) * count, count, axis=2)
-
-    tables = jnp.concatenate(
-        [small_piece(0)] + [swap(small_piece(m), m) for m in (1, 2, 3)], axis=1
-    )
-    table_rows = tables[:3].astype(jnp.int32)
-    table_scale = tables[3:]
-    weights = [
-        [piece(v, 0)] + [swap(piece(v, m), m) for m in (1, 2, 3)]
-        for v in (gate_values, up_values, down_values)
-    ]
-    grads, own, other = columns(table_rows, table_scale, near, far, weights, mine)
-
-    def home(pieces):
-        result = jnp.zeros((per_dev, local_cols, blk, blk), bf)
-        for m, part in enumerate(pieces):
-            part = part if m == 0 else swap(part, m)
-            result = lax.dynamic_update_slice_in_dim(result, part, (mine ^ m) * count, axis=1)
-        return result
-
-    grad_gate, grad_up, grad_down = [home(p) for p in grads]
+    small = small.reshape(6, per_dev, 4, count).transpose(2, 0, 1, 3)
+    own_w = (gate_values, up_values, down_values)
+    tok_all, *recv_w, table = gather(small, both, own_w, shards)
+    kept = lax.dynamic_slice_in_dim(small, mine, 1, axis=0)
+    table = jnp.concatenate([kept, table]).transpose(1, 0, 2, 3).reshape(6, 4 * per_dev, count)
+    table_rows = table[:3].astype(jnp.int32)
+    table_scale = table[3:]
+    results = [jnp.zeros((per_dev, local_cols, blk, blk), bf) for _ in own_w]
+    prev, base = (), 0
+    first = max(1, count * SPLIT // 10)
+    chunks = []
+    for size in (first, count - first):
+        if size:
+            grads, prev = columns(table_rows, table_scale, mine.reshape(1), tok_all, own_w, recv_w, base, size, prev)
+            sent = [[p if m == 0 else swap(p, m) for m, p in enumerate(pieces)] for pieces in grads]
+            chunks.append((base, sent))
+            base += size
+    for base, sent in chunks:
+        for i, pieces in enumerate(sent):
+            for m, part in enumerate(pieces):
+                results[i] = lax.dynamic_update_slice_in_dim(
+                    results[i], part, (mine ^ m) * count + base, axis=1
+                )
+    own, other = prev
     chip = (own.astype(f32) + swap(other, 1).astype(f32)).astype(bf)
     shard = lax.psum_scatter(chip, "tensor", scatter_dimension=0, tiled=False)
     done = (shard[:, 0].astype(f32) + swap(shard[:, 1], 2).astype(f32)).astype(bf)
     done = done.transpose(0, 2, 1, 3).reshape(2, tok, width)
-    return (done[0], done[1], grad_gate, grad_up, grad_down)
+    return (done[0], done[1], *results)
 
 
 def choose_plan(mesh, *args):
-    shards, columns_here = mesh.shape["fsdp"], args[2].shape[1]
-    plan = exchanged_plan if shards == 4 and columns_here % shards == 0 else gathered_plan
+    fits = mesh.shape["fsdp"] == 4 and mesh.shape["parts"] == 2 and args[2].shape[0] == 2
+    fits = fits and args[2].shape[1] % 4 == 0
+    plan = exchanged_plan if fits else gathered_plan
     return plan(*args)
 
 

time: 375 us -> 285 us (0.76)
  waiting for transfers between devices: 250 us -> 77.7 us
  Pallas kernels: 51.4 us -> 146 us
  local copies, waits for them, and re-layouts: 30.3 us -> 21.9 us
  starting transfers between devices: 20.8 us -> 14.8 us
    all_gather x1 -> x0, waiting for transfers between devices: 82.3 us -> none  [exchanged_plan(): near = lax.all_gather(both, 'tensor', axis=0)]
    pallas_call x0 -> x1, Pallas kernels: none -> 77.2 us  [gather(): pl.pallas_call(functools.partial(gather_kernel, shards), out_shape=[jax.S...]
    ppermute x25 -> x20, waiting for transfers between devices: 128 us -> 68.1 us  [swap(): return lax.ppermute(value, 'fsdp', [(i, i ^ flip) for i in range(4)])]
    reduce_scatter x1, waiting for transfers between devices: 39.9 us -> 9.6 us  [exchanged_plan(): shard = lax.psum_scatter(chip, 'tensor', scatter_dimension=0, tiled=False)]
    pallas_call x1 -> x2, Pallas kernels: 51.4 us -> 68.7 us  [columns(): pl.pallas_call(functools.partial(column_kernel, (slots, per_dev, nblk, bl...]
    ppermute x25 -> x20, starting transfers between devices: 20.8 us -> 14.7 us  [swap(): return lax.ppermute(value, 'fsdp', [(i, i ^ flip) for i in range(4)])]
    dynamic_slice x4 -> x1, local copies, waits for them, and re-layouts: 5.21 us -> 0.01 us  [exchanged_plan(): kept = lax.dynamic_slice_in_dim(small, mine, 1, axis=0)]
    dynamic_update_slice x12 -> x23, local copies, waits for them, and re-layouts: 12.5 us -> 10.2 us  [exchanged_plan(): lax.dynamic_update_slice_in_dim(results[i], part, (mine ^ m) * count + ba...]
  transfers between devices with their start and end apart: 27 -> 21, of which waited for: 14 -> 10; matrix products, arithmetic and copies ran while one was open for 7% -> 5% of each run, Pallas kernels for 0% -> 0%
where the time goes in v2:
time: 285 us
  Pallas kernels  146 us (51%)
  waiting for transfers between devices  77.7 us (27%)
  local copies, waits for them, and re-layouts  21.9 us (8%)
  starting transfers between devices  14.8 us (5%)
  between operations  14.6 us (5%)
  other arithmetic  9.83 us (3%)
    pallas_call x1, Pallas kernels, gather(): pl.pallas_call(functools.partial(gather_kernel, shards), out_shape=[jax.S...  77.2 us
    pallas_call x2, Pallas kernels, columns(): pl.pallas_call(functools.partial(column_kernel, (slots, per_dev, nblk, bl...  68.7 us
    ppermute x20, waiting for transfers between devices, swap(): return lax.ppermute(value, 'fsdp', [(i, i ^ flip) for i in range(4)])  68.1 us
    ppermute x20, starting transfers between devices, swap(): return lax.ppermute(value, 'fsdp', [(i, i ^ flip) for i in range(4)])  14.7 us
    dynamic_update_slice x23, local copies, waits for them, and re-layouts, exchanged_plan(): lax.dynamic_update_slice_in_dim(results[i], part, (mine ^ m) * count + ba...  10.2 us
    reduce_scatter x1, waiting for transfers between devices, exchanged_plan(): shard = lax.psum_scatter(chip, 'tensor', scatter_dimension=0, tiled=False)  9.6 us
    convert_element_type x1, other arithmetic, exchanged_plan(): chip = (own.astype(f32) + swap(other, 1).astype(f32)).astype(bf)  6.05 us
  transfers between devices with their start and end apart: 21, of which 10 were waited for; matrix products, arithmetic and copies ran while one was open for 5% of the time, Pallas kernels for 0%

profile of v2, /device:TPU:0, one launch (start us, length us, event | category | flops | bytes accessed | tf_op | source)
XLA Modules:
  0.0 284.8 jit_solution(1802005882280244227)
XLA Ops:
  7.2 0.7 convert_element_type.38
  7.9 0.1 stack.36
  8.0 0.7 convert_element_type.39
  8.7 0.1 stack.37
  8.8 0.7 convert_element_type.40
  9.4 0.1 stack.38
  9.5 0.7 reshape.48
  10.3 0.7 reshape.49
  11.0 0.7 reshape.50
  11.7 1.1 copy.49
  12.9 0.2 copy.51
  13.1 1.1 copy.48
  14.2 0.2 copy.50
  14.5 0.8 maximum_bitcast_fusion.both
  15.3 77.2 %shard_map.146 = (bf16[2,4,2,2,8,128,128]{6,5,4,3,2,1,0:T(8,128)(2,1)}, bf16[3,2,10,128,128]{4,3,2,1,0:T(8,128)(2,1)}, bf16[3,2,10,128,128]{4,3,2,1,0:T(8,128)(2...) custom-call(f32[4,6,2,10]{3,2,1,0:T(2,128)} %bitcast.32, bf16[2,8,128,128]{3,2,1,0:T(8,128)(2,1)} %maximum_bitcast_fusion.both, ...), custom_call_target="tpu_custom_call" | custom-call | tf_op jit(solution)/shard_map/pallas_call | solution.py:294
  92.5 0.7 maximum_bitcast_fusion.1
  93.3 0.6 copy.52
  93.9 0.6 copy.53
  94.5 31.7 %shard_map.147 = (bf16[2,5,128,128]{3,2,1,0:T(8,128)(2,1)}, bf16[2,5,128,128]{3,2,1,0:T(8,128)(2,1)}, bf16[2,5,128,128]{3,2,1,0:T(8,128)(2,1)}, bf16[2,5,128,128...) custom-call(s32[3,8,10]{2,1,0:T(8,128)} %bitcast.33, ...), custom_call_target="tpu_custom_call" | custom-call | flops 12079595520 | bytes 41943040 | tf_op jit(solution)/shard_map/pallas_call | solution.py:424
  126.2 37.0 %shard_map.148 = (bf16[2,5,128,128]{3,2,1,0:T(8,128)(2,1)}, bf16[2,5,128,128]{3,2,1,0:T(8,128)(2,1)}, bf16[2,5,128,128]{3,2,1,0:T(8,128)(2,1)}, bf16[2,5,128,128...) custom-call(s32[3,8,10]{2,1,0:T(8,128)} %bitcast.34, ...), custom_call_target="tpu_custom_call" | custom-call | flops 12079595520 | bytes 41943040 | tf_op jit(solution)/shard_map/pallas_call | solution.py:424
  163.2 0.4 collective-permute-start
  163.7 7.0 %collective-permute-done = bf16[4,2,2,8,128,128]{5,4,3,2,1,0:T(8,128)(2,1)S(1)} collective-permute-done((bf16[4,2,2,8,128,128]{5,4,3,2,1,0:T(8,128)(2,1)}, bf16[4,2,2,8,128,128]{5,4,3,2,1,0:T(8,128)(2,1)S(1)}, u32[]{:S(2)}, u32[]{:S(2)}) %collective-permute-start) | collective-permute-done | bytes 4194336 | tf_op jit(solution)/shard_map/ppermute | solution.py:451
  170.7 6.0 %add_convert_fusion = bf16[4,2,2,8,128,128]{5,4,3,2,1,0:T(8,128)(2,1)} fusion(bf16[4,2,2,8,128,128]{5,4,3,2,1,0:T(8,128)(2,1)S(1)} %collective-permute-done, bf16[4,2,2,8,128,128]{5,4,3,2,1,0:T(8,128)(2,1)} %get-tuple-element.45), kind=kLoop, calls=%fused_computation | loop fusion | flops 8388608 | bytes 12582912 | tf_op jit(solution)/shard_map/convert_element_type | solution.py:502
  176.8 0.4 collective-permute-start.2
  177.2 1.5 collective-permute-start.3
  178.7 0.6 collective-permute-start.14
  179.3 0.6 broadcast.3.clone
  180.1 0.6 broadcast.3.clone.1
  180.8 0.6 broadcast.3.clone.2
  181.6 0.1 copy-done.18
  181.7 1.5 collective-permute-start.15
  183.2 1.1 constant_dynamic-update-slice_fusion.28
  184.3 0.6 collective-permute-start.9
  184.9 1.0 constant_dynamic-update-slice_fusion.12
  185.9 1.1 collective-permute-start.16
  187.1 1.0 constant_dynamic-update-slice_fusion.20
  188.1 13.9 %collective-permute-done.15 = bf16[2,5,128,128]{3,2,1,0:T(8,128)(2,1)S(1)} collective-permute-done((bf16[2,5,128,128]{3,2,1,0:T(8,128)(2,1)S(1)}, bf16[2,5,128,128]{3,2,1,0:T(8,128)(2,1)S(1)}, u32[]{:S(2)}, u32[]{:S(2)}) %collective-permute-start.15) | collective-permute-done | bytes 327712 | tf_op jit(solution)/shard_map/ppermute | solution.py:451
  202.1 7.0 %collective-permute-done.9 = bf16[2,5,128,128]{3,2,1,0:T(8,128)(2,1)S(1)} collective-permute-done((bf16[2,5,128,128]{3,2,1,0:T(8,128)(2,1)S(1)}, bf16[2,5,128,128]{3,2,1,0:T(8,128)(2,1)S(1)}, u32[]{:S(2)}, u32[]{:S(2)}) %collective-permute-start.9) | collective-permute-done | bytes 327712 | tf_op jit(solution)/shard_map/ppermute | solution.py:451
  209.1 6.0 %collective-permute-done.16 = bf16[2,5,128,128]{3,2,1,0:T(8,128)(2,1)S(1)} collective-permute-done((bf16[2,5,128,128]{3,2,1,0:T(8,128)(2,1)S(1)}, bf16[2,5,128,128]{3,2,1,0:T(8,128)(2,1)S(1)}, u32[]{:S(2)}, u32[]{:S(2)}) %collective-permute-start.16) | collective-permute-done | bytes 327712 | tf_op jit(solution)/shard_map/ppermute | solution.py:451
  215.1 0.8 collective-permute-start.6
  215.9 6.2 %collective-permute-done.10 = bf16[2,5,128,128]{3,2,1,0:T(8,128)(2,1)S(1)} collective-permute-done((bf16[2,5,128,128]{3,2,1,0:T(8,128)(2,1)S(1)}, bf16[2,5,128,128]{3,2,1,0:T(8,128)(2,1)S(1)}, u32[]{:S(2)}, u32[]{:S(2)}) %collective-permute-start.10) | collective-permute-done | bytes 327712 | tf_op jit(solution)/shard_map/ppermute | solution.py:451
  222.1 2.3 collective-permute-start.7
  224.5 0.1 constant_dynamic-update-slice_fusion.9
  224.6 0.1 collective-permute-start.11
  224.8 0.6 collective-permute-start.12
  225.5 1.4 collective-permute-start.13
  226.9 0.4 collective-permute-start.17
  227.3 2.8 collective-permute-done.6
  230.1 1.5 collective-permute-start.18
  231.7 12.5 %collective-permute-done.12 = bf16[2,5,128,128]{3,2,1,0:T(8,128)(2,1)S(1)} collective-permute-done((bf16[2,5,128,128]{3,2,1,0:T(8,128)(2,1)S(1)}, bf16[2,5,128,128]{3,2,1,0:T(8,128)(2,1)S(1)}, u32[]{:S(2)}, u32[]{:S(2)}) %collective-permute-start.12) | collective-permute-done | bytes 327712 | tf_op jit(solution)/shard_map/ppermute | solution.py:451
  244.2 9.6 %reduce-scatter.2.cloned.1.call-done = bf16[1,2,2,8,128,128]{5,4,3,2,1,0:T(8,128)(2,1)} async-done(((bf16[4,2,2,8,128,128]{5,4,3,2,1,0:T(8,128)(2,1)}), bf16[1,2,2,8,128,128]{5,4,3,2,1,0:T(8,128)(2,1)}) %reduce-scatter.2.cloned.1.call-update) | async-done | bytes 1048592 | tf_op jit(solution)/shard_map/reduce_scatter | solution.py:503
  253.8 1.2 slice_bitcast_fusion
  255.0 1.5 collective-permute-start.1
  256.5 1.8 constant_dynamic-update-slice_fusion.22
  258.3 0.9 constant_dynamic-update-slice_fusion.8
  259.2 1.8 constant_dynamic-update-slice_fusion.7
  261.1 3.2 %collective-permute-done.19 = bf16[2,5,128,128]{3,2,1,0:T(8,128)(2,1)} collective-permute-done((bf16[2,5,128,128]{3,2,1,0:T(8,128)(2,1)}, bf16[2,5,128,128]{3,2,1,0:T(8,128)(2,1)}, u32[]{:S(2)}, u32[]{:S(2)}) %collective-permute-start.19) | collective-permute-done | bytes 327712 | tf_op jit(solution)/shard_map/ppermute | solution.py:451
  264.3 1.8 constant_dynamic-update-slice_fusion.6
  266.1 9.6 %collective-permute-done.1 = bf16[2,8,128,128]{3,2,1,0:T(8,128)(2,1)S(1)} collective-permute-done((bf16[2,8,128,128]{3,2,1,0:T(8,128)(2,1)S(1)}, bf16[2,8,128,128]{3,2,1,0:T(8,128)(2,1)S(1)}, u32[]{:S(2)}, u32[]{:S(2)}) %collective-permute-start.1) | collective-permute-done | bytes 524320 | tf_op jit(solution)/shard_map/ppermute | solution.py:451
  275.6 0.1 fusion.1
  275.8 0.2 copy.55
  276.0 0.9 copy.57
  276.9 0.2 copy.56
  277.1 0.9 copy.58
  (79 shorter events, 1.0 us)
Async XLA Ops:
  7.2 246.7 %reduce-scatter.2.cloned.1.call-start = ((), (), s32[]{:S(2)}) async-start(), calls=%async_computation.1 | async-start | bytes 5242880 | tf_op jit(solution)/shard_map/reduce_scatter | solution.py:503
  14.4 0.9 copy-start.10
  163.2 7.4 %collective-permute-start = (bf16[4,2,2,8,128,128]{5,4,3,2,1,0:T(8,128)(2,1)}, bf16[4,2,2,8,128,128]{5,4,3,2,1,0:T(8,128)(2,1)S(1)}, u32[]{:S(2)}, u32[]{:S(2)}) collective-permute-start(bf16[4,2,2,8,128,128]{5,4,3,2,1,0:T(8,128)(2,1)} %get-tuple-element.46), channel_id=1, source_target_pairs={{0,1},{1,0},{2,3},{3,2},{4,5},{5,4},{6,7},{7,6},{8,9},{9,8},{10,11... | collective-permute-start | bytes 12582920 | tf_op jit(solution)/shard_map/ppermute | solution.py:451
  176.7 3.2 %copy-start.7 = (bf16[2,5,128,128]{3,2,1,0:T(8,128)(2,1)S(1)}, bf16[2,5,128,128]{3,2,1,0:T(8,128)(2,1)}, u32[]{:S(2)}) copy-start(bf16[2,5,128,128]{3,2,1,0:T(8,128)(2,1)} %get-tuple-element.47) | copy-start | bytes 983044
  176.8 4.8 %collective-permute-start.2 = (bf16[2,5,128,128]{3,2,1,0:T(8,128)(2,1)}, bf16[2,5,128,128]{3,2,1,0:T(8,128)(2,1)}, u32[]{:S(2)}, u32[]{:S(2)}) collective-permute-start(bf16[2,5,128,128]{3,2,1,0:T(8,128)(2,1)} %get-tuple-element.48), channel_id=1, source_target_pairs={{0,1},{1,0},{2,3},{3,2},{4,5},{5,4},{6,7},{7,6},{8,9},{9,8},{10,11... | collective-permute-start | bytes 983048 | tf_op jit(solution)/shard_map/ppermute | solution.py:451
  177.2 47.4 %collective-permute-start.3 = (bf16[2,5,128,128]{3,2,1,0:T(8,128)(2,1)}, bf16[2,5,128,128]{3,2,1,0:T(8,128)(2,1)S(1)}, u32[]{:S(2)}, u32[]{:S(2)}) collective-permute-start(bf16[2,5,128,128]{3,2,1,0:T(8,128)(2,1)} %get-tuple-element.49), channel_id=1, source_target_pairs={{0,2},{1,3},{2,0},{3,1},{4,6},{5,7},{6,4},{7,5},{8,10},{9,11},{10,... | collective-permute-start | bytes 983048 | tf_op jit(solution)/shard_map/ppermute | solution.py:451
  178.7 46.1 %collective-permute-start.4 = (bf16[2,5,128,128]{3,2,1,0:T(8,128)(2,1)}, bf16[2,5,128,128]{3,2,1,0:T(8,128)(2,1)S(1)}, u32[]{:S(2)}, u32[]{:S(2)}) collective-permute-start(bf16[2,5,128,128]{3,2,1,0:T(8,128)(2,1)} %get-tuple-element.50), channel_id=1, source_target_pairs={{0,3},{1,2},{2,1},{3,0},{4,7},{5,6},{6,5},{7,4},{8,11},{9,10},{10,... | collective-permute-start | bytes 983048 | tf_op jit(solution)/shard_map/ppermute | solution.py:451
  178.7 5.6 %collective-permute-start.14 = (bf16[2,5,128,128]{3,2,1,0:T(8,128)(2,1)}, bf16[2,5,128,128]{3,2,1,0:T(8,128)(2,1)}, u32[]{:S(2)}, u32[]{:S(2)}) collective-permute-start(bf16[2,5,128,128]{3,2,1,0:T(8,128)(2,1)} %get-tuple-element.64), channel_id=1, source_target_pairs={{0,1},{1,0},{2,3},{3,2},{4,5},{5,4},{6,7},{7,6},{8,9},{9,8},{10,11... | collective-permute-start | bytes 983048 | tf_op jit(solution)/shard_map/ppermute | solution.py:451
  179.3 6.6 %collective-permute-start.8 = (bf16[2,5,128,128]{3,2,1,0:T(8,128)(2,1)}, bf16[2,5,128,128]{3,2,1,0:T(8,128)(2,1)}, u32[]{:S(2)}, u32[]{:S(2)}) collective-permute-start(bf16[2,5,128,128]{3,2,1,0:T(8,128)(2,1)} %get-tuple-element.56), channel_id=1, source_target_pairs={{0,1},{1,0},{2,3},{3,2},{4,5},{5,4},{6,7},{7,6},{8,9},{9,8},{10,11... | collective-permute-start | bytes 983048 | tf_op jit(solution)/shard_map/ppermute | solution.py:451
  179.3 1.4 copy-start.6
  180.0 1.4 copy-start.5
  180.7 1.0 copy-start.18
  180.7 3.6 %copy-start.17 = (bf16[2,5,128,128]{3,2,1,0:T(8,128)(2,1)S(1)}, bf16[2,5,128,128]{3,2,1,0:T(8,128)(2,1)}, u32[]{:S(2)}) copy-start(bf16[2,5,128,128]{3,2,1,0:T(8,128)(2,1)} %get-tuple-element.57) | copy-start | bytes 983044
  180.7 5.2 %copy-start.16 = (bf16[2,5,128,128]{3,2,1,0:T(8,128)(2,1)S(1)}, bf16[2,5,128,128]{3,2,1,0:T(8,128)(2,1)}, u32[]{:S(2)}) copy-start(bf16[2,5,128,128]{3,2,1,0:T(8,128)(2,1)} %get-tuple-element.66) | copy-start | bytes 983044
  180.8 21.2 %copy-start.15 = (bf16[2,5,128,128]{3,2,1,0:T(8,128)(2,1)S(1)}, bf16[2,5,128,128]{3,2,1,0:T(8,128)(2,1)}, u32[]{:S(2)}) copy-start(bf16[2,5,128,128]{3,2,1,0:T(8,128)(2,1)} %get-tuple-element.58) | copy-start | bytes 983044
  180.8 28.3 %copy-start.14 = (bf16[2,5,128,128]{3,2,1,0:T(8,128)(2,1)S(1)}, bf16[2,5,128,128]{3,2,1,0:T(8,128)(2,1)}, u32[]{:S(2)}) copy-start(bf16[2,5,128,128]{3,2,1,0:T(8,128)(2,1)} %get-tuple-element.52) | copy-start | bytes 983044
  181.5 33.6 %copy-start.12 = (bf16[2,5,128,128]{3,2,1,0:T(8,128)(2,1)S(1)}, bf16[2,5,128,128]{3,2,1,0:T(8,128)(2,1)}, u32[]{:S(2)}) copy-start(bf16[2,5,128,128]{3,2,1,0:T(8,128)(2,1)} %get-tuple-element.53) | copy-start | bytes 983044
  181.5 43.0 %copy-start.8 = (bf16[2,5,128,128]{3,2,1,0:T(8,128)(2,1)S(1)}, bf16[2,5,128,128]{3,2,1,0:T(8,128)(2,1)}, u32[]{:S(2)}) copy-start(bf16[2,5,128,128]{3,2,1,0:T(8,128)(2,1)} %get-tuple-element.59) | copy-start | bytes 983044
  181.5 43.0 %copy-start.9 = (bf16[2,5,128,128]{3,2,1,0:T(8,128)(2,1)S(1)}, bf16[2,5,128,128]{3,2,1,0:T(8,128)(2,1)}, u32[]{:S(2)}) copy-start(bf16[2,5,128,128]{3,2,1,0:T(8,128)(2,1)} %get-tuple-element.67) | copy-start | bytes 983044
  181.7 20.3 %collective-permute-start.15 = (bf16[2,5,128,128]{3,2,1,0:T(8,128)(2,1)S(1)}, bf16[2,5,128,128]{3,2,1,0:T(8,128)(2,1)S(1)}, u32[]{:S(2)}, u32[]{:S(2)}) collective-permute-start(bf16[2,5,128,128]{3,2,1,0:T(8,128)(2,1)S(1)} %copy-done.18), channel_id=1, source_target_pairs={{0,2},{1,3},{2,0},{3,1},{4,6},{5,7},{6,4},{7,5},{8,10},{9,11},{10,... | collective-permute-start | bytes 983048 | tf_op jit(solution)/shard_map/ppermute | solution.py:451
  184.3 40.3 %copy-start.13 = (bf16[2,5,128,128]{3,2,1,0:T(8,128)(2,1)S(1)}, bf16[2,5,128,128]{3,2,1,0:T(8,128)(2,1)}, u32[]{:S(2)}) copy-start(bf16[2,5,128,128]{3,2,1,0:T(8,128)(2,1)} %get-tuple-element.60) | copy-start | bytes 983044
  184.3 24.7 %collective-permute-start.9 = (bf16[2,5,128,128]{3,2,1,0:T(8,128)(2,1)S(1)}, bf16[2,5,128,128]{3,2,1,0:T(8,128)(2,1)S(1)}, u32[]{:S(2)}, u32[]{:S(2)}) collective-permute-start(bf16[2,5,128,128]{3,2,1,0:T(8,128)(2,1)S(1)} %copy-done.17), channel_id=1, source_target_pairs={{0,2},{1,3},{2,0},{3,1},{4,6},{5,7},{6,4},{7,5},{8,10},{9,11},{10,... | collective-permute-start | bytes 983048 | tf_op jit(solution)/shard_map/ppermute | solution.py:451
  185.9 38.8 %copy-start.11 = (bf16[2,5,128,128]{3,2,1,0:T(8,128)(2,1)S(1)}, bf16[2,5,128,128]{3,2,1,0:T(8,128)(2,1)}, u32[]{:S(2)}) copy-start(bf16[2,5,128,128]{3,2,1,0:T(8,128)(2,1)} %get-tuple-element.61) | copy-start | bytes 983044
  185.9 29.1 %collective-permute-start.16 = (bf16[2,5,128,128]{3,2,1,0:T(8,128)(2,1)S(1)}, bf16[2,5,128,128]{3,2,1,0:T(8,128)(2,1)S(1)}, u32[]{:S(2)}, u32[]{:S(2)}) collective-permute-start(bf16[2,5,128,128]{3,2,1,0:T(8,128)(2,1)S(1)} %copy-done.16), channel_id=1, source_target_pairs={{0,3},{1,2},{2,1},{3,0},{4,7},{5,6},{6,5},{7,4},{8,11},{9,10},{10,... | collective-permute-start | bytes 983048 | tf_op jit(solution)/shard_map/ppermute | solution.py:451
  202.0 23.4 %copy-start.4 = (bf16[2,5,128,128]{3,2,1,0:T(8,128)(2,1)S(1)}, bf16[2,5,128,128]{3,2,1,0:T(8,128)(2,1)}, u32[]{:S(2)}) copy-start(bf16[2,5,128,128]{3,2,1,0:T(8,128)(2,1)} %get-tuple-element.51) | copy-start | bytes 983044
  202.0 20.1 %collective-permute-start.10 = (bf16[2,5,128,128]{3,2,1,0:T(8,128)(2,1)S(1)}, bf16[2,5,128,128]{3,2,1,0:T(8,128)(2,1)S(1)}, u32[]{:S(2)}, u32[]{:S(2)}) collective-permute-start(bf16[2,5,128,128]{3,2,1,0:T(8,128)(2,1)S(1)} %copy-done.15), channel_id=1, source_target_pairs={{0,3},{1,2},{2,1},{3,0},{4,7},{5,6},{6,5},{7,4},{8,11},{9,10},{10,... | collective-permute-start | bytes 983048 | tf_op jit(solution)/shard_map/ppermute | solution.py:451
  209.1 16.5 %collective-permute-start.5 = (bf16[2,5,128,128]{3,2,1,0:T(8,128)(2,1)S(1)}, bf16[2,5,128,128]{3,2,1,0:T(8,128)(2,1)S(1)}, u32[]{:S(2)}, u32[]{:S(2)}) collective-permute-start(bf16[2,5,128,128]{3,2,1,0:T(8,128)(2,1)S(1)} %copy-done.14), channel_id=1, source_target_pairs={{0,1},{1,0},{2,3},{3,2},{4,5},{5,4},{6,7},{7,6},{8,9},{9,8},{10,11... | collective-permute-start | bytes 983048 | tf_op jit(solution)/shard_map/ppermute | solution.py:451
  215.1 15.0 %collective-permute-start.6 = (bf16[2,5,128,128]{3,2,1,0:T(8,128)(2,1)S(1)}, bf16[2,5,128,128]{3,2,1,0:T(8,128)(2,1)S(1)}, u32[]{:S(2)}, u32[]{:S(2)}) collective-permute-start(bf16[2,5,128,128]{3,2,1,0:T(8,128)(2,1)S(1)} %copy-done.12), channel_id=1, source_target_pairs={{0,2},{1,3},{2,0},{3,1},{4,6},{5,7},{6,4},{7,5},{8,10},{9,11},{10,... | collective-permute-start | bytes 983048 | tf_op jit(solution)/shard_map/ppermute | solution.py:451
  222.1 32.9 %collective-permute-start.7 = (bf16[2,5,128,128]{3,2,1,0:T(8,128)(2,1)}, bf16[2,5,128,128]{3,2,1,0:T(8,128)(2,1)}, u32[]{:S(2)}, u32[]{:S(2)}) collective-permute-start(bf16[2,5,128,128]{3,2,1,0:T(8,128)(2,1)} %get-tuple-element.54), channel_id=1, source_target_pairs={{0,3},{1,2},{2,1},{3,0},{4,7},{5,6},{6,5},{7,4},{8,11},{9,10},{10,... | collective-permute-start | bytes 983048 | tf_op jit(solution)/shard_map/ppermute | solution.py:451
  224.6 19.6 %copy-start.2 = (bf16[2,40,128,128]{3,2,1,0:T(8,128)(2,1)}, bf16[2,40,128,128]{3,2,1,0:T(8,128)(2,1)S(1)}, u32[]{:S(2)}) copy-start(bf16[2,40,128,128]{3,2,1,0:T(8,128)(2,1)S(1)} %get-tuple-element.85) | copy-start | bytes 7864324
  224.6 2.3 collective-permute-start.11
  224.8 19.4 %collective-permute-start.12 = (bf16[2,5,128,128]{3,2,1,0:T(8,128)(2,1)S(1)}, bf16[2,5,128,128]{3,2,1,0:T(8,128)(2,1)S(1)}, u32[]{:S(2)}, u32[]{:S(2)}) collective-permute-start(bf16[2,5,128,128]{3,2,1,0:T(8,128)(2,1)S(1)} %copy-done.11), channel_id=1, source_target_pairs={{0,2},{1,3},{2,0},{3,1},{4,6},{5,7},{6,4},{7,5},{8,10},{9,11},{10,... | collective-permute-start | bytes 983048 | tf_op jit(solution)/shard_map/ppermute | solution.py:451
  225.5 32.8 %collective-permute-start.13 = (bf16[2,5,128,128]{3,2,1,0:T(8,128)(2,1)}, bf16[2,5,128,128]{3,2,1,0:T(8,128)(2,1)S(1)}, u32[]{:S(2)}, u32[]{:S(2)}) collective-permute-start(bf16[2,5,128,128]{3,2,1,0:T(8,128)(2,1)} %get-tuple-element.62), channel_id=1, source_target_pairs={{0,3},{1,2},{2,1},{3,0},{4,7},{5,6},{6,5},{7,4},{8,11},{9,10},{10,... | collective-permute-start | bytes 983048 | tf_op jit(solution)/shard_map/ppermute | solution.py:451
  226.9 31.4 %collective-permute-start.17 = (bf16[2,5,128,128]{3,2,1,0:T(8,128)(2,1)}, bf16[2,5,128,128]{3,2,1,0:T(8,128)(2,1)S(1)}, u32[]{:S(2)}, u32[]{:S(2)}) collective-permute-start(bf16[2,5,128,128]{3,2,1,0:T(8,128)(2,1)} %get-tuple-element.68), channel_id=1, source_target_pairs={{0,1},{1,0},{2,3},{3,2},{4,5},{5,4},{6,7},{7,6},{8,9},{9,8},{10,11... | collective-permute-start | bytes 983048 | tf_op jit(solution)/shard_map/ppermute | solution.py:451
  230.1 29.1 %collective-permute-start.18 = (bf16[2,5,128,128]{3,2,1,0:T(8,128)(2,1)}, bf16[2,5,128,128]{3,2,1,0:T(8,128)(2,1)}, u32[]{:S(2)}, u32[]{:S(2)}) collective-permute-start(bf16[2,5,128,128]{3,2,1,0:T(8,128)(2,1)} %get-tuple-element.69), channel_id=1, source_target_pairs={{0,2},{1,3},{2,0},{3,1},{4,6},{5,7},{6,4},{7,5},{8,10},{9,11},{10,... | collective-permute-start | bytes 983048 | tf_op jit(solution)/shard_map/ppermute | solution.py:451
  231.6 12.5 %copy-start.1 = (bf16[2,40,128,128]{3,2,1,0:T(8,128)(2,1)}, bf16[2,40,128,128]{3,2,1,0:T(8,128)(2,1)S(1)}, u32[]{:S(2)}) copy-start(bf16[2,40,128,128]{3,2,1,0:T(8,128)(2,1)S(1)} %constant_dynamic-update-slice_fusion.23) | copy-start | bytes 7864324
  244.2 20.2 %collective-permute-start.19 = (bf16[2,5,128,128]{3,2,1,0:T(8,128)(2,1)}, bf16[2,5,128,128]{3,2,1,0:T(8,128)(2,1)}, u32[]{:S(2)}, u32[]{:S(2)}) collective-permute-start(bf16[2,5,128,128]{3,2,1,0:T(8,128)(2,1)} %get-tuple-element.70), channel_id=1, source_target_pairs={{0,3},{1,2},{2,1},{3,0},{4,7},{5,6},{6,5},{7,4},{8,11},{9,10},{10,... | collective-permute-start | bytes 983048 | tf_op jit(solution)/shard_map/ppermute | solution.py:451
  253.8 21.8 %copy-start.3 = (bf16[1,2,2,8,128,128]{5,4,3,2,1,0:T(8,128)(2,1)S(1)}, bf16[1,2,2,8,128,128]{5,4,3,2,1,0:T(8,128)(2,1)}, u32[]{:S(2)}) copy-start(bf16[1,2,2,8,128,128]{5,4,3,2,1,0:T(8,128)(2,1)} %reduce-scatter.2.cloned.1.call-done) | copy-start | bytes 3145732
  255.0 20.6 %collective-permute-start.1 = (bf16[2,8,128,128]{3,2,1,0:T(8,128)(2,1)S(1)}, bf16[2,8,128,128]{3,2,1,0:T(8,128)(2,1)S(1)}, u32[]{:S(2)}, u32[]{:S(2)}) collective-permute-start(bf16[2,8,128,128]{3,2,1,0:T(8,128)(2,1)S(1)} %slice_bitcast_fusion), channel_id=1, source_target_pairs={{0,2},{1,3},{2,0},{3,1},{4,6},{5,7},{6,4},{7,5},{8,10},{9,11},{10,... | collective-permute-start | bytes 1572872 | tf_op jit(solution)/shard_map/ppermute | solution.py:451
  258.3 18.5 %copy-start = (bf16[2,40,128,128]{3,2,1,0:T(8,128)(2,1)}, bf16[2,40,128,128]{3,2,1,0:T(8,128)(2,1)S(1)}, u32[]{:S(2)}) copy-start(bf16[2,40,128,128]{3,2,1,0:T(8,128)(2,1)S(1)} %constant_dynamic-update-slice_fusion.14) | copy-start | bytes 7864324
Sparse Core Ops, SparseCore 0:
  176.9 76.8 reduce-scatter.1

commit v3 on v2

--- a/solution.py
+++ b/solution.py
@@ -140,9 +140,6 @@
         .astype(jnp.bfloat16)
     )
     return (layer_out, grad_tokens, grad_gate, grad_up, grad_down)
-
-
-SPLIT = 5
 
 
 def gather_kernel(shards, small, both, wg, wu, wd, tok_all, rg, ru, rd, table, *sems):
@@ -305,39 +302,26 @@
     )(small, both, *weights)
 
 
-def column_kernel(
-    shape,
-    rows_ref,
-    scale_ref,
-    mine_ref,
-    tok_ref,
-    *refs,
-):
-    slots, per_dev, nblk, blk, tok, base, nprev = shape
+def column_kernel(shape, backward, rows_ref, scale_ref, mine_ref, tok_ref, *refs):
+    slots, per_dev, nblk, blk, tok = shape
     nsrc = slots // per_dev
-    prev_refs, refs = refs[:nprev], refs[nprev:]
-    own_w, recv_w = refs[:3], refs[3:6]
-    grad_refs = [refs[6 + i * nsrc : 6 + (1 + i) * nsrc] for i in range(3)]
-    own_ref, other_ref = refs[3 * nsrc + 6 : 3 * nsrc + 8]
-    (out_acc, in_acc, gate_sel, up_sel, down_sel, gate_w, up_w, down_w) = refs[3 * nsrc + 8 :]
-    step = pl.program_id(0)
-    r = step + base
+    own_w, recv_w, refs = refs[:3], refs[3:6], refs[6:]
+    if backward:
+        gate_pre_ref, up_pre_ref = refs[:2]
+        grad_refs = [refs[2 : 2 + nsrc], refs[2 + nsrc : 2 + 2 * nsrc], ()]
+        own_ref, other_ref = refs[2 + 2 * nsrc : 4 + 2 * nsrc]
+        scratch = refs[4 + 2 * nsrc :]
+    else:
+        grad_refs = [(), (), refs[:nsrc]]
+        gate_pre_ref, up_pre_ref, own_ref, other_ref = refs[nsrc : nsrc + 4]
+        scratch = refs[nsrc + 4 :]
+    acc, gate_sel, up_sel, down_sel, gate_w, up_w, down_w = scratch
+    r = pl.program_id(0)
     per_shard = tok_ref.shape[4]
 
-    @pl.when(step == 0)
+    @pl.when(r == 0)
     def _():
-        if not nprev:
-            out_acc[...] = jnp.zeros_like(out_acc)
-            in_acc[...] = jnp.zeros_like(in_acc)
-            return
-        for which, acc in enumerate((out_acc, in_acc)):
-            for c, ref in enumerate(prev_refs):
-                for x in range(2):
-                    q = c * 2 + x
-
-                    @pl.loop(0, nblk)
-                    def _(d):
-                        acc[d, q * tok : (q + 1) * tok, :] = ref[d // per_shard, which, x, d % per_shard].astype(jnp.float32)
+        acc[...] = jnp.zeros_like(acc)
 
     def load(which, slot, array, sel):
         place = rows_ref[array, slot, r]
@@ -365,72 +349,79 @@
     nn = (((1,), (0,)), ((), ()))
     nt = (((1,), (1,)), ((), ()))
     dot = functools.partial(lax.dot_general, preferred_element_type=jnp.float32)
-    gate_pre = dot(gate_sel[...], gate_w[...], nn)
-    up_pre = dot(up_sel[...], up_w[...], nn)
-    grad_hidden = dot(down_sel[...], down_w[...], nt)
-    sig = jax.nn.sigmoid(gate_pre)
-    act = gate_pre * sig
-    hidden = (act * up_pre).astype(jnp.bfloat16)
-    gate_act = (grad_hidden * up_pre * sig * (1.0 + gate_pre * (1.0 - sig))).astype(jnp.bfloat16)
-    up_act = (grad_hidden * act).astype(jnp.bfloat16)
-
-    for slot in range(slots):
-        span = slice(slot * blk, (slot + 1) * blk)
-        src, sub = slot // per_dev, slot % per_dev
-        g = dot(gate_sel[:, span].T, gate_act, nn) * scale_ref[0, slot, r]
-        grad_refs[0][src][sub, 0] = g.astype(jnp.bfloat16)
-        g = dot(up_sel[:, span].T, up_act, nn) * scale_ref[1, slot, r]
-        grad_refs[1][src][sub, 0] = g.astype(jnp.bfloat16)
-    hidden_t = hidden.T
-    down = dot(hidden_t, down_sel[...], nn)
-    for slot in range(slots):
-        src, sub = slot // per_dev, slot % per_dev
-        g = down[:, slot * blk : (slot + 1) * blk] * scale_ref[2, slot, r]
-        grad_refs[2][src][sub, 0] = g.astype(jnp.bfloat16)
-
-    for array, acc, left, w in ((0, in_acc, gate_act, gate_w), (1, in_acc, up_act, up_w), (2, out_acc, hidden, down_w)):
-        product = dot(left, w[...], nn if array == 2 else nt)
+
+    def add(array, left, w, form):
+        product = dot(left, w[...], form)
         for slot in range(slots):
-            place = rows_ref[array, slot, r]
-            acc[place] += product[:, slot * blk : (slot + 1) * blk]
-
-    @pl.when(step == pl.num_programs(0) - 1)
+            acc[rows_ref[array, slot, r]] += product[:, slot * blk : (slot + 1) * blk]
+
+    if backward:
+        gate_pre, up_pre = gate_pre_ref[0], up_pre_ref[0]
+        grad_hidden = dot(down_sel[...], down_w[...], nt)
+        sig = jax.nn.sigmoid(gate_pre)
+        act = gate_pre * sig
+        gate_act = (grad_hidden * up_pre * sig * (1.0 + gate_pre * (1.0 - sig))).astype(jnp.bfloat16)
+        up_act = (grad_hidden * act).astype(jnp.bfloat16)
+        for slot in range(slots):
+            span = slice(slot * blk, (slot + 1) * blk)
+            src, sub = slot // per_dev, slot % per_dev
+            g = dot(gate_sel[:, span].T, gate_act, nn) * scale_ref[0, slot, r]
+            grad_refs[0][src][sub, 0] = g.astype(jnp.bfloat16)
+            g = dot(up_sel[:, span].T, up_act, nn) * scale_ref[1, slot, r]
+            grad_refs[1][src][sub, 0] = g.astype(jnp.bfloat16)
+        add(0, gate_act, gate_w, nt)
+        add(1, up_act, up_w, nt)
+    else:
+        gate_pre = dot(gate_sel[...], gate_w[...], nn)
+        up_pre = dot(up_sel[...], up_w[...], nn)
+        gate_pre_ref[0], up_pre_ref[0] = gate_pre, up_pre
+        hidden = (gate_pre * jax.nn.sigmoid(gate_pre) * up_pre).astype(jnp.bfloat16)
+        down = dot(hidden.T, down_sel[...], nn)
+        for slot in range(slots):
+            src, sub = slot // per_dev, slot % per_dev
+            g = down[:, slot * blk : (slot + 1) * blk] * scale_ref[2, slot, r]
+            grad_refs[2][src][sub, 0] = g.astype(jnp.bfloat16)
+        add(2, hidden, down_w, nn)
+
+    @pl.when(r == pl.num_programs(0) - 1)
     def _():
-        for which, acc in enumerate((out_acc, in_acc)):
-            for c, ref in enumerate((own_ref, other_ref)):
-                for x in range(2):
-                    q = c * 2 + x
-
-                    @pl.loop(0, nblk)
-                    def _(d):
-                        ref[d // per_shard, which, x, d % per_shard] = acc[d, q * tok : (q + 1) * tok, :].astype(jnp.bfloat16)
-
-
-def columns(table_rows, table_scale, mine, tok_all, own_w, recv_w, base, size, prev):
+        for c, ref in enumerate((own_ref, other_ref)):
+            for x in range(2):
+                q = c * 2 + x
+
+                @pl.loop(0, nblk)
+                def _(d):
+                    ref[d // per_shard, x, d % per_shard] = acc[d, q * tok : (q + 1) * tok, :].astype(jnp.bfloat16)
+
+
+def columns(table_rows, table_scale, mine, tok_all, own_w, recv_w, kept):
     nsrc = 1 + recv_w[0].shape[0]
     _, per_dev, count, blk, _ = recv_w[0].shape
     _, shards, _, _, per_shard, tok, _ = tok_all.shape
     nblk = shards * per_shard
     slots = per_dev * nsrc
     total = 4 * tok
+    bf, f32 = jnp.bfloat16, jnp.float32
     whole = lambda a: pl.BlockSpec(a, lambda r, *_: (0,) * len(a), pipeline_mode=pl.Buffered(1))
-    own_block = pl.BlockSpec((per_dev, 1, blk, blk), lambda r, rows, scale, at: (0, at[0] * count + base + r, 0, 0))
-    recv_block = pl.BlockSpec((nsrc - 1, per_dev, 1, blk, blk), lambda r, *_: (0, 0, base + r, 0, 0))
+    own_block = pl.BlockSpec((per_dev, 1, blk, blk), lambda r, rows, scale, at: (0, at[0] * count + r, 0, 0))
+    recv_block = pl.BlockSpec((nsrc - 1, per_dev, 1, blk, blk), lambda r, *_: (0, 0, r, 0, 0))
     block = pl.BlockSpec((per_dev, 1, blk, blk), lambda r, *_: (0, r, 0, 0))
-    piece = jax.ShapeDtypeStruct((per_dev, size, blk, blk), jnp.bfloat16)
-    out_block = (shards, 2, 2, per_shard, tok, blk)
-    bf = jnp.bfloat16
-    flops = 2 * 9 * slots * size * total * blk * blk
-    outs = pl.pallas_call(
-        functools.partial(column_kernel, (slots, per_dev, nblk, blk, tok, base, len(prev))),
+    piece = jax.ShapeDtypeStruct((per_dev, count, blk, blk), bf)
+    pre_block = [pl.BlockSpec((1, total, blk), lambda r, *_: (r, 0, 0))] * 2
+    pre = [jax.ShapeDtypeStruct((count, total, blk), f32)] * 2
+    out_block = (shards, 2, per_shard, tok, blk)
+    sums = [jax.ShapeDtypeStruct(out_block, bf)] * 2
+    backward = len(kept) > 0
+    flops = 2 * 9 * slots * count * total * blk * blk
+    return pl.pallas_call(
+        functools.partial(column_kernel, (slots, per_dev, nblk, blk, tok), backward),
         grid_spec=pltpu.PrefetchScalarGridSpec(
             num_scalar_prefetch=3,
-            grid=(size,),
-            in_specs=[whole(tok_all.shape)] + [whole(out_block)] * len(prev) + [own_block] * 3 + [recv_block] * 3,
-            out_specs=[block] * (3 * nsrc) + [whole(out_block)] * 2,
+            grid=(count,),
+            in_specs=[whole(tok_all.shape)] + [own_block] * 3 + [recv_block] * 3 + (pre_block if backward else []),
+            out_specs=([block] * (2 * nsrc) if backward else [block] * nsrc + pre_block) + [whole(out_block)] * 2,
             scratch_shapes=[
-                pltpu.VMEM((nblk, total, blk), jnp.float32),
-                pltpu.VMEM((nblk, total, blk), jnp.float32),
+                pltpu.VMEM((nblk, total, blk), f32),
                 pltpu.VMEM((total, slots * blk), bf),
                 pltpu.VMEM((total, slots * blk), bf),
                 pltpu.VMEM((total, slots * blk), bf),
@@ -439,12 +430,10 @@
                 pltpu.VMEM((blk, slots * blk), bf),
             ],
         ),
-        out_shape=[piece] * (3 * nsrc) + [jax.ShapeDtypeStruct(out_block, bf)] * 2,
+        out_shape=([piece] * (2 * nsrc) if backward else [piece] * nsrc + pre) + sums,
         compiler_params=pltpu.CompilerParams(vmem_limit_bytes=60 * 1024 * 1024),
-        cost_estimate=pl.CostEstimate(flops=2 * flops, bytes_accessed=40 << 20, transcendentals=0),
-    )(table_rows, table_scale, mine, tok_all, *prev, *own_w, *recv_w)
-    grads = [outs[i * nsrc : (i + 1) * nsrc] for i in range(3)]
-    return grads, outs[3 * nsrc :]
+        cost_estimate=pl.CostEstimate(flops=flops, bytes_accessed=40 << 20, transcendentals=0),
+    )(table_rows, table_scale, mine, tok_all, *own_w, *recv_w, *kept)
 
 
 def swap(value, flip):
@@ -482,28 +471,36 @@
     table = jnp.concatenate([kept, table]).transpose(1, 0, 2, 3).reshape(6, 4 * per_dev, count)
     table_rows = table[:3].astype(jnp.int32)
     table_scale = table[3:]
-    results = [jnp.zeros((per_dev, local_cols, blk, blk), bf) for _ in own_w]
-    prev, base = (), 0
-    first = max(1, count * SPLIT // 10)
-    chunks = []
-    for size in (first, count - first):
-        if size:
-            grads, prev = columns(table_rows, table_scale, mine.reshape(1), tok_all, own_w, recv_w, base, size, prev)
-            sent = [[p if m == 0 else swap(p, m) for m, p in enumerate(pieces)] for pieces in grads]
-            chunks.append((base, sent))
-            base += size
-    for base, sent in chunks:
-        for i, pieces in enumerate(sent):
-            for m, part in enumerate(pieces):
-                results[i] = lax.dynamic_update_slice_in_dim(
-                    results[i], part, (mine ^ m) * count + base, axis=1
-                )
-    own, other = prev
-    chip = (own.astype(f32) + swap(other, 1).astype(f32)).astype(bf)
-    shard = lax.psum_scatter(chip, "tensor", scatter_dimension=0, tiled=False)
-    done = (shard[:, 0].astype(f32) + swap(shard[:, 1], 2).astype(f32)).astype(bf)
-    done = done.transpose(0, 2, 1, 3).reshape(2, tok, width)
-    return (done[0], done[1], *results)
+
+    def home(pieces):
+        result = jnp.zeros((per_dev, local_cols, blk, blk), bf)
+        for m, part in enumerate(pieces):
+            result = lax.dynamic_update_slice_in_dim(result, part, (mine ^ m) * count, axis=1)
+        return result
+
+    def send(pieces):
+        return [p if m == 0 else swap(p, m) for m, p in enumerate(pieces)]
+
+    def chip_sum(own, other):
+        return (own.astype(f32) + swap(other, 1).astype(f32)).astype(bf)
+
+    def scatter(chip):
+        return lax.psum_scatter(chip, "tensor", scatter_dimension=0, tiled=False)
+
+    def finish(shard):
+        total = (shard[0].astype(f32) + swap(shard[1], 2).astype(f32)).astype(bf)
+        return total.transpose(1, 0, 2).reshape(tok, width)
+
+    place = mine.reshape(1)
+    *down_pieces, gate_pre, up_pre, own, other = columns(table_rows, table_scale, place, tok_all, own_w, recv_w, ())
+    chip = chip_sum(own, other)
+    down_sent = send(down_pieces)
+    chip, table_scale = lax.optimization_barrier((chip, table_scale))
+    out_shard = scatter(chip)
+    late = columns(table_rows, table_scale, place, tok_all, own_w, recv_w, (gate_pre, up_pre))
+    gate_sent, up_sent = send(late[:4]), send(late[4:8])
+    in_shard = scatter(chip_sum(late[8], late[9]))
+    return (finish(out_shard), finish(in_shard), home(gate_sent), home(up_sent), home(down_sent))
 
 
 def choose_plan(mesh, *args):

time: 285 us -> 284 us (level)
  Pallas kernels: 146 us -> 141 us
  waiting for transfers between devices: 77.7 us -> 82.7 us
  starting transfers between devices: 14.8 us -> 10.2 us
  other arithmetic: 9.83 us -> 13.2 us
    ppermute x20 -> x13, waiting for transfers between devices: 68.1 us -> 82.6 us  [swap(): return lax.ppermute(value, 'fsdp', [(i, i ^ flip) for i in range(4)])]
    reduce_scatter x1 -> x2, waiting for transfers between devices: 9.6 us -> 0.02 us  [scatter(): return lax.psum_scatter(chip, 'tensor', scatter_dimension=0, tiled=False)]
    pallas_call x2, Pallas kernels: 68.7 us -> 63.7 us  [columns(): pl.pallas_call(functools.partial(column_kernel, (slots, per_dev, nblk, bl...]
    ppermute x20 -> x13, starting transfers between devices: 14.7 us -> 9.92 us  [swap(): return lax.ppermute(value, 'fsdp', [(i, i ^ flip) for i in range(4)])]
    dynamic_update_slice x23 -> x12, local copies, waits for them, and re-layouts: 10.2 us -> 6.61 us  [home(): lax.dynamic_update_slice_in_dim(result, part, (mine ^ m) * count, axis=1)]
    convert_element_type x1 -> x2, other arithmetic: 6.05 us -> 7.57 us  [chip_sum(): return (own.astype(f32) + swap(other, 1).astype(f32)).astype(bf)]
    unnamed x47 -> x25, local copies, waits for them, and re-layouts: 4.22 us -> 5.74 us
  transfers between devices with their start and end apart: 21 -> 15, of which waited for: 10 -> 10; matrix products, arithmetic and copies ran while one was open for 5% -> 6% of each run, Pallas kernels for 0% -> 13%
where the time goes in v3:
time: 284 us; the launch traced here: 283 us
  Pallas kernels  141 us (50%)
  waiting for transfers between devices  82.7 us (29%)
  local copies, waits for them, and re-layouts  21.3 us (8%)
  between operations  14.4 us (5%)
  other arithmetic  13.2 us (5%)
  starting transfers between devices  10.2 us (4%)
    ppermute x13, waiting for transfers between devices, swap(): return lax.ppermute(value, 'fsdp', [(i, i ^ flip) for i in range(4)])  82.6 us
    pallas_call x1, Pallas kernels, gather(): pl.pallas_call(functools.partial(gather_kernel, shards), out_shape=[jax.S...  77.2 us
    pallas_call x2, Pallas kernels, columns(): pl.pallas_call(functools.partial(column_kernel, (slots, per_dev, nblk, bl...  63.7 us
    ppermute x13, starting transfers between devices, swap(): return lax.ppermute(value, 'fsdp', [(i, i ^ flip) for i in range(4)])  9.92 us
    convert_element_type x2, other arithmetic, chip_sum(): return (own.astype(f32) + swap(other, 1).astype(f32)).astype(bf)  7.57 us
    dynamic_update_slice x12, local copies, waits for them, and re-layouts, home(): lax.dynamic_update_slice_in_dim(result, part, (mine ^ m) * count, axis=1)  6.61 us
    unnamed x25, local copies, waits for them, and re-layouts  5.74 us
  transfers between devices with their start and end apart: 15, of which 10 were waited for; matrix products, arithmetic and copies ran while one was open for 6% of the time, Pallas kernels for 13%

profile of v3, /device:TPU:0, one launch (start us, length us, event | category | flops | bytes accessed | tf_op | source)
XLA Modules:
  0.0 282.7 jit_solution(2933042635476993677)
XLA Ops:
  7.2 0.7 convert_element_type.59
  8.0 0.7 convert_element_type.60
  8.8 0.7 convert_element_type.61
  9.5 0.7 reshape.60
  10.3 0.7 reshape.61
  11.0 0.7 reshape.62
  11.7 1.1 copy.47
  12.9 0.2 copy.49
  13.1 1.1 copy.46
  14.2 0.2 copy.48
  14.5 0.8 maximum_bitcast_fusion.both
  15.3 77.2 %shard_map.146 = (bf16[2,4,2,2,8,128,128]{6,5,4,3,2,1,0:T(8,128)(2,1)}, bf16[3,2,10,128,128]{4,3,2,1,0:T(8,128)(2,1)}, bf16[3,2,10,128,128]{4,3,2,1,0:T(8,128)(2...) custom-call(f32[4,6,2,10]{3,2,1,0:T(2,128)} %bitcast.36, bf16[2,8,128,128]{3,2,1,0:T(8,128)(2,1)} %maximum_bitcast_fusion.both, ...), custom_call_target="tpu_custom_call" | custom-call | tf_op jit(solution)/shard_map/pallas_call | solution.py:291
  92.5 0.7 maximum_bitcast_fusion.1
  93.3 0.6 copy.50
  93.9 0.6 copy.51
  94.5 26.0 %shard_map.147 = (bf16[2,10,128,128]{3,2,1,0:T(8,128)(2,1)}, bf16[2,10,128,128]{3,2,1,0:T(8,128)(2,1)}, bf16[2,10,128,128]{3,2,1,0:T(8,128)(2,1)}, bf16[2,10,128...) custom-call(s32[3,8,10]{2,1,0:T(8,128)} %bitcast.37, ...), custom_call_target="tpu_custom_call" | custom-call | flops 12079595520 | bytes 41943040 | tf_op jit(solution)/shard_map/pallas_call | solution.py:416
  120.5 0.4 collective-permute-start
  120.9 4.0 %collective-permute-done = bf16[4,2,8,128,128]{4,3,2,1,0:T(8,128)(2,1)S(1)} collective-permute-done((bf16[4,2,8,128,128]{4,3,2,1,0:T(8,128)(2,1)}, bf16[4,2,8,128,128]{4,3,2,1,0:T(8,128)(2,1)S(1)}, u32[]{:S(2)}, u32[]{:S(2)}) %collective-permute-start) | collective-permute-done | bytes 2097184 | tf_op jit(solution)/shard_map/ppermute | solution.py:440
  124.9 3.8 %add_convert_fusion.1 = bf16[4,2,8,128,128]{4,3,2,1,0:T(8,128)(2,1)} fusion(bf16[4,2,8,128,128]{4,3,2,1,0:T(8,128)(2,1)S(1)} %collective-permute-done, bf16[4,2,8,128,128]{4,3,2,1,0:T(8,128)(2,1)} %get-tuple-element.35), kind=kLoop, calls=%fused_computation.1 | loop fusion | flops 4194304 | bytes 6291456 | tf_op jit(solution)/shard_map/convert_element_type | solution.py:485
  128.8 0.2 reduce-scatter.5.cloned.1.call-start
  129.0 37.7 %shard_map.148 = (bf16[2,10,128,128]{3,2,1,0:T(8,128)(2,1)}, bf16[2,10,128,128]{3,2,1,0:T(8,128)(2,1)}, bf16[2,10,128,128]{3,2,1,0:T(8,128)(2,1)}, bf16[2,10,128...) custom-call(s32[3,8,10]{2,1,0:T(8,128)} %bitcast.38, ...), custom_call_target="tpu_custom_call" | custom-call | flops 12079595520 | bytes 41943040 | tf_op jit(solution)/shard_map/pallas_call | solution.py:416
  166.7 0.4 collective-permute-start.2
  167.1 4.0 %collective-permute-done.2 = bf16[4,2,8,128,128]{4,3,2,1,0:T(8,128)(2,1)S(1)} collective-permute-done((bf16[4,2,8,128,128]{4,3,2,1,0:T(8,128)(2,1)}, bf16[4,2,8,128,128]{4,3,2,1,0:T(8,128)(2,1)S(1)}, u32[]{:S(2)}, u32[]{:S(2)}) %collective-permute-start.2) | collective-permute-done | bytes 2097184 | tf_op jit(solution)/shard_map/ppermute | solution.py:440
  171.1 3.7 %add_convert_fusion = bf16[4,2,8,128,128]{4,3,2,1,0:T(8,128)(2,1)} fusion(bf16[4,2,8,128,128]{4,3,2,1,0:T(8,128)(2,1)S(1)} %collective-permute-done.2, bf16[4,2,8,128,128]{4,3,2,1,0:T(8,128)(2,1)} %get-tuple-element.41), kind=kLoop, calls=%fused_computation | loop fusion | flops 4194304 | bytes 6291456 | tf_op jit(solution)/shard_map/convert_element_type | solution.py:485
  174.9 0.5 collective-permute-start.10
  175.4 1.5 collective-permute-start.11
  176.9 0.7 collective-permute-start.4
  177.5 0.6 broadcast.3.clone.2
  178.1 1.2 constant_dynamic-update-slice_fusion.9
  179.4 1.5 collective-permute-start.5
  180.9 1.2 constant_dynamic-update-slice_fusion.8
  182.3 11.0 %collective-permute-done.11 = bf16[2,10,128,128]{3,2,1,0:T(8,128)(2,1)} collective-permute-done((bf16[2,10,128,128]{3,2,1,0:T(8,128)(2,1)}, bf16[2,10,128,128]{3,2,1,0:T(8,128)(2,1)}, u32[]{:S(2)}, u32[]{:S(2)}) %collective-permute-start.11) | collective-permute-done | bytes 655392 | tf_op jit(solution)/shard_map/ppermute | solution.py:440
  193.3 1.2 constant_dynamic-update-slice_fusion.7
  194.6 11.7 %collective-permute-done.12 = bf16[2,10,128,128]{3,2,1,0:T(8,128)(2,1)} collective-permute-done((bf16[2,10,128,128]{3,2,1,0:T(8,128)(2,1)}, bf16[2,10,128,128]{3,2,1,0:T(8,128)(2,1)}, u32[]{:S(2)}, u32[]{:S(2)}) %collective-permute-start.12) | collective-permute-done | bytes 655392 | tf_op jit(solution)/shard_map/ppermute | solution.py:440
  206.3 1.2 constant_dynamic-update-slice_fusion.6
  207.5 0.8 collective-permute-start.8
  208.4 0.6 broadcast.3.clone
  209.0 0.1 constant_dynamic-update-slice_fusion.17
  209.1 0.6 broadcast.3.clone.1
  209.8 0.3 copy-done.3
  210.1 0.1 constant_dynamic-update-slice_fusion.13
  210.2 1.8 collective-permute-start.9
  212.0 0.1 constant_dynamic-update-slice_fusion.16
  212.1 9.1 %collective-permute-done.5 = bf16[2,10,128,128]{3,2,1,0:T(8,128)(2,1)S(1)} collective-permute-done((bf16[2,10,128,128]{3,2,1,0:T(8,128)(2,1)}, bf16[2,10,128,128]{3,2,1,0:T(8,128)(2,1)S(1)}, u32[]{:S(2)}, u32[]{:S(2)}) %collective-permute-start.5) | collective-permute-done | bytes 655392 | tf_op jit(solution)/shard_map/ppermute | solution.py:440
  221.3 0.1 constant_dynamic-update-slice_fusion.15
  221.4 13.1 %collective-permute-done.6 = bf16[2,10,128,128]{3,2,1,0:T(8,128)(2,1)S(1)} collective-permute-done((bf16[2,10,128,128]{3,2,1,0:T(8,128)(2,1)}, bf16[2,10,128,128]{3,2,1,0:T(8,128)(2,1)S(1)}, u32[]{:S(2)}, u32[]{:S(2)}) %collective-permute-start.6) | collective-permute-done | bytes 655392 | tf_op jit(solution)/shard_map/ppermute | solution.py:440
  234.4 0.1 constant_dynamic-update-slice_fusion.14
  234.5 0.1 constant_dynamic-update-slice_fusion.12
  234.6 1.4 copy-done.2
  236.0 13.4 %collective-permute-done.8 = bf16[2,10,128,128]{3,2,1,0:T(8,128)(2,1)S(1)} collective-permute-done((bf16[2,10,128,128]{3,2,1,0:T(8,128)(2,1)S(1)}, bf16[2,10,128,128]{3,2,1,0:T(8,128)(2,1)S(1)}, u32[]{:S(2)}, u32[]{:S(2)}) %collective-permute-start.8) | collective-permute-done | bytes 655392 | tf_op jit(solution)/shard_map/ppermute | solution.py:440
  249.5 1.0 slice_bitcast_fusion.2
  250.5 1.5 collective-permute-start.1
  252.0 1.7 slice_bitcast_fusion
  253.7 0.6 collective-permute-start.3
  254.2 8.3 %collective-permute-done.9 = bf16[2,10,128,128]{3,2,1,0:T(8,128)(2,1)} collective-permute-done((bf16[2,10,128,128]{3,2,1,0:T(8,128)(2,1)}, bf16[2,10,128,128]{3,2,1,0:T(8,128)(2,1)}, u32[]{:S(2)}, u32[]{:S(2)}) %collective-permute-start.9) | collective-permute-done | bytes 655392 | tf_op jit(solution)/shard_map/ppermute | solution.py:440
  262.5 1.2 constant_dynamic-update-slice_fusion.10
  263.7 5.3 %collective-permute-done.1 = bf16[8,128,128]{2,1,0:T(8,128)(2,1)S(1)} collective-permute-done((bf16[8,128,128]{2,1,0:T(8,128)(2,1)S(1)}, bf16[8,128,128]{2,1,0:T(8,128)(2,1)S(1)}, u32[]{:S(2)}, u32[]{:S(2)}) %collective-permute-start.1) | collective-permute-done | bytes 262176 | tf_op jit(solution)/shard_map/ppermute | solution.py:440
  269.0 1.0 fusion.2
  270.1 0.2 copy.52
  270.2 0.9 copy.54
  271.1 2.7 collective-permute-done.3
  273.8 1.0 fusion.3
  274.8 0.2 copy.53
  275.0 0.9 copy.55
  (37 shorter events, 0.7 us)
Async XLA Ops:
  7.2 242.3 %reduce-scatter.3.cloned.1.call-start = ((), (), s32[]{:S(2)}) async-start(), calls=%async_computation.2 | async-start | bytes 2621440 | tf_op jit(solution)/shard_map/reduce_scatter | solution.py:488
  14.4 0.9 copy-start.5
  120.5 4.4 %collective-permute-start = (bf16[4,2,8,128,128]{4,3,2,1,0:T(8,128)(2,1)}, bf16[4,2,8,128,128]{4,3,2,1,0:T(8,128)(2,1)S(1)}, u32[]{:S(2)}, u32[]{:S(2)}) collective-permute-start(bf16[4,2,8,128,128]{4,3,2,1,0:T(8,128)(2,1)} %get-tuple-element.36), channel_id=1, source_target_pairs={{0,1},{1,0},{2,3},{3,2},{4,5},{5,4},{6,7},{7,6},{8,9},{9,8},{10,11... | collective-permute-start | bytes 6291464 | tf_op jit(solution)/shard_map/ppermute | solution.py:440
  128.8 123.2 %reduce-scatter.5.cloned.1.call-start = ((), (), s32[]{:S(2)}) async-start(), calls=%async_computation.3 | async-start | bytes 2621440 | tf_op jit(solution)/shard_map/reduce_scatter | solution.py:488
  166.7 4.4 %collective-permute-start.2 = (bf16[4,2,8,128,128]{4,3,2,1,0:T(8,128)(2,1)}, bf16[4,2,8,128,128]{4,3,2,1,0:T(8,128)(2,1)S(1)}, u32[]{:S(2)}, u32[]{:S(2)}) collective-permute-start(bf16[4,2,8,128,128]{4,3,2,1,0:T(8,128)(2,1)} %get-tuple-element.42), channel_id=1, source_target_pairs={{0,1},{1,0},{2,3},{3,2},{4,5},{5,4},{6,7},{7,6},{8,9},{9,8},{10,11... | collective-permute-start | bytes 6291464 | tf_op jit(solution)/shard_map/ppermute | solution.py:440
  174.9 6.0 %collective-permute-start.10 = (bf16[2,10,128,128]{3,2,1,0:T(8,128)(2,1)}, bf16[2,10,128,128]{3,2,1,0:T(8,128)(2,1)}, u32[]{:S(2)}, u32[]{:S(2)}) collective-permute-start(bf16[2,10,128,128]{3,2,1,0:T(8,128)(2,1)} %get-tuple-element.52), channel_id=1, source_target_pairs={{0,1},{1,0},{2,3},{3,2},{4,5},{5,4},{6,7},{7,6},{8,9},{9,8},{10,11... | collective-permute-start | bytes 1966088 | tf_op jit(solution)/shard_map/ppermute | solution.py:440
  175.4 17.9 %collective-permute-start.11 = (bf16[2,10,128,128]{3,2,1,0:T(8,128)(2,1)}, bf16[2,10,128,128]{3,2,1,0:T(8,128)(2,1)}, u32[]{:S(2)}, u32[]{:S(2)}) collective-permute-start(bf16[2,10,128,128]{3,2,1,0:T(8,128)(2,1)} %get-tuple-element.53), channel_id=1, source_target_pairs={{0,2},{1,3},{2,0},{3,1},{4,6},{5,7},{6,4},{7,5},{8,10},{9,11},{10,... | collective-permute-start | bytes 1966088 | tf_op jit(solution)/shard_map/ppermute | solution.py:440
  176.8 29.5 %collective-permute-start.12 = (bf16[2,10,128,128]{3,2,1,0:T(8,128)(2,1)}, bf16[2,10,128,128]{3,2,1,0:T(8,128)(2,1)}, u32[]{:S(2)}, u32[]{:S(2)}) collective-permute-start(bf16[2,10,128,128]{3,2,1,0:T(8,128)(2,1)} %get-tuple-element.54), channel_id=1, source_target_pairs={{0,3},{1,2},{2,1},{3,0},{4,7},{5,6},{6,5},{7,4},{8,11},{9,10},{10,... | collective-permute-start | bytes 1966088 | tf_op jit(solution)/shard_map/ppermute | solution.py:440
  176.9 33.4 %collective-permute-start.4 = (bf16[2,10,128,128]{3,2,1,0:T(8,128)(2,1)}, bf16[2,10,128,128]{3,2,1,0:T(8,128)(2,1)S(1)}, u32[]{:S(2)}, u32[]{:S(2)}) collective-permute-start(bf16[2,10,128,128]{3,2,1,0:T(8,128)(2,1)} %get-tuple-element.44), channel_id=1, source_target_pairs={{0,1},{1,0},{2,3},{3,2},{4,5},{5,4},{6,7},{7,6},{8,9},{9,8},{10,11... | collective-permute-start | bytes 1966088 | tf_op jit(solution)/shard_map/ppermute | solution.py:440
  179.4 15.1 %copy-start.7 = (bf16[2,10,128,128]{3,2,1,0:T(8,128)(2,1)S(1)}, bf16[2,10,128,128]{3,2,1,0:T(8,128)(2,1)}, u32[]{:S(2)}) copy-start(bf16[2,10,128,128]{3,2,1,0:T(8,128)(2,1)} %get-tuple-element.48) | copy-start | bytes 1966084
  179.4 28.2 %copy-start.6 = (bf16[2,10,128,128]{3,2,1,0:T(8,128)(2,1)S(1)}, bf16[2,10,128,128]{3,2,1,0:T(8,128)(2,1)}, u32[]{:S(2)}) copy-start(bf16[2,10,128,128]{3,2,1,0:T(8,128)(2,1)} %get-tuple-element.49) | copy-start | bytes 1966084
  179.4 41.9 %collective-permute-start.5 = (bf16[2,10,128,128]{3,2,1,0:T(8,128)(2,1)}, bf16[2,10,128,128]{3,2,1,0:T(8,128)(2,1)S(1)}, u32[]{:S(2)}, u32[]{:S(2)}) collective-permute-start(bf16[2,10,128,128]{3,2,1,0:T(8,128)(2,1)} %get-tuple-element.45), channel_id=1, source_target_pairs={{0,2},{1,3},{2,0},{3,1},{4,6},{5,7},{6,4},{7,5},{8,10},{9,11},{10,... | collective-permute-start | bytes 1966088 | tf_op jit(solution)/shard_map/ppermute | solution.py:440
  182.2 26.8 %copy-start.4 = (bf16[2,10,128,128]{3,2,1,0:T(8,128)(2,1)S(1)}, bf16[2,10,128,128]{3,2,1,0:T(8,128)(2,1)}, u32[]{:S(2)}) copy-start(bf16[2,10,128,128]{3,2,1,0:T(8,128)(2,1)} %get-tuple-element.43) | copy-start | bytes 1966084
  182.2 52.2 %collective-permute-start.6 = (bf16[2,10,128,128]{3,2,1,0:T(8,128)(2,1)}, bf16[2,10,128,128]{3,2,1,0:T(8,128)(2,1)S(1)}, u32[]{:S(2)}, u32[]{:S(2)}) collective-permute-start(bf16[2,10,128,128]{3,2,1,0:T(8,128)(2,1)} %get-tuple-element.46), channel_id=1, source_target_pairs={{0,3},{1,2},{2,1},{3,0},{4,7},{5,6},{6,5},{7,4},{8,11},{9,10},{10,... | collective-permute-start | bytes 1966088 | tf_op jit(solution)/shard_map/ppermute | solution.py:440
  194.5 40.0 %collective-permute-start.7 = (bf16[2,10,128,128]{3,2,1,0:T(8,128)(2,1)S(1)}, bf16[2,10,128,128]{3,2,1,0:T(8,128)(2,1)S(1)}, u32[]{:S(2)}, u32[]{:S(2)}) collective-permute-start(bf16[2,10,128,128]{3,2,1,0:T(8,128)(2,1)S(1)} %copy-done.7), channel_id=1, source_target_pairs={{0,1},{1,0},{2,3},{3,2},{4,5},{5,4},{6,7},{7,6},{8,9},{9,8},{10,11... | collective-permute-start | bytes 1966088 | tf_op jit(solution)/shard_map/ppermute | solution.py:440
  207.5 1.6 copy-start.1
  207.5 41.8 %collective-permute-start.8 = (bf16[2,10,128,128]{3,2,1,0:T(8,128)(2,1)S(1)}, bf16[2,10,128,128]{3,2,1,0:T(8,128)(2,1)S(1)}, u32[]{:S(2)}, u32[]{:S(2)}) collective-permute-start(bf16[2,10,128,128]{3,2,1,0:T(8,128)(2,1)S(1)} %copy-done.6), channel_id=1, source_target_pairs={{0,2},{1,3},{2,0},{3,1},{4,6},{5,7},{6,4},{7,5},{8,10},{9,11},{10,... | collective-permute-start | bytes 1966088 | tf_op jit(solution)/shard_map/ppermute | solution.py:440
  209.0 1.1 copy-start.3
  210.2 52.3 %collective-permute-start.9 = (bf16[2,10,128,128]{3,2,1,0:T(8,128)(2,1)}, bf16[2,10,128,128]{3,2,1,0:T(8,128)(2,1)}, u32[]{:S(2)}, u32[]{:S(2)}) collective-permute-start(bf16[2,10,128,128]{3,2,1,0:T(8,128)(2,1)} %get-tuple-element.50), channel_id=1, source_target_pairs={{0,3},{1,2},{2,1},{3,0},{4,7},{5,6},{6,5},{7,4},{8,11},{9,10},{10,... | collective-permute-start | bytes 1966088 | tf_op jit(solution)/shard_map/ppermute | solution.py:440
  234.5 1.5 copy-start.2
  250.5 18.6 %collective-permute-start.1 = (bf16[8,128,128]{2,1,0:T(8,128)(2,1)S(1)}, bf16[8,128,128]{2,1,0:T(8,128)(2,1)S(1)}, u32[]{:S(2)}, u32[]{:S(2)}) collective-permute-start(bf16[8,128,128]{2,1,0:T(8,128)(2,1)S(1)} %slice_bitcast_fusion.2), channel_id=1, source_target_pairs={{0,2},{1,3},{2,0},{3,1},{4,6},{5,7},{6,4},{7,5},{8,10},{9,11},{10,... | collective-permute-start | bytes 786440 | tf_op jit(solution)/shard_map/ppermute | solution.py:440
  253.7 20.1 %collective-permute-start.3 = (bf16[8,128,128]{2,1,0:T(8,128)(2,1)}, bf16[8,128,128]{2,1,0:T(8,128)(2,1)S(1)}, u32[]{:S(2)}, u32[]{:S(2)}) collective-permute-start(bf16[8,128,128]{2,1,0:T(8,128)(2,1)} %slice_bitcast_fusion), channel_id=1, source_target_pairs={{0,2},{1,3},{2,0},{3,1},{4,6},{5,7},{6,4},{7,5},{8,10},{9,11},{10,... | collective-permute-start | bytes 786440 | tf_op jit(solution)/shard_map/ppermute | solution.py:440
  263.7 12.1 %copy-start = (bf16[2,40,128,128]{3,2,1,0:T(8,128)(2,1)}, bf16[2,40,128,128]{3,2,1,0:T(8,128)(2,1)S(1)}, u32[]{:S(2)}) copy-start(bf16[2,40,128,128]{3,2,1,0:T(8,128)(2,1)S(1)} %constant_dynamic-update-slice_fusion.10) | copy-start | bytes 7864324
Sparse Core Ops, SparseCore 0:
  128.9 43.7 reduce-scatter.2
  175.6 43.2 reduce-scatter.4
